TPU v7x, 32 devices: a whole 2x2x4 slice. The times are simulated.
32 devices in a mesh: grp: 2 (over y), chan: 4 (over z), tm: 2 (over x), sub: 2 (over core).
Axes of the slice: x: 2, y: 2, z: 4, core: 2. Of those that a mesh axis runs over, the one named last changes fastest.
Arguments:
- raw: bfloat16 [1024, 16384], P(('grp', 'chan'), ('tm', 'sub')), parts along dimension 0, may hold values from -6 to 6
- fir_taps: bfloat16 [129], replicated, may hold values from -0.5 to 0.5
- spatial_taps: float32 [9], replicated, may hold values from -2 to 2
- band_edges: int32 [4], replicated, may hold values from 1 to 125, as said below
- source_owner: int32 [16], P('grp'), parts along dimension 0, may hold values from 0 to 3
- source_panel: int32 [8], replicated, may hold values from 0 to 3
- source_pick: int32 [8, 1024], P(None, ('grp', 'chan')), parts along dimension 1, may hold values from 0 to 31
Outputs:
- correlations: float32 [8, 1024, 128], P(None, ('grp', 'chan')), parts along dimension 1
There are 2 independent parts, one for each index of `grp`. A program takes and returns all parts, laid end to end along the dimension named above; an argument that names none is the same for every part. Nothing has to cross between parts.
Inputs may be any that keep to these rules, and one draw needn't show every extreme that they name: `band_edges`: e0 < e1 <= e2 < e3, with e1 - e0 and e3 - e2 from 4 to 12.
All inputs are finite; a program needn't handle non-finite values.
Results may differ from a plain program's by a relative error of at most 0.0055.
Values may be sent and summed in bfloat16 or wider, within the bound.
A program may use at most 64 MiB of HBM per device.

v0:
```python
import math

import jax
import jax.numpy as jnp
from jax import lax
from jax.sharding import PartitionSpec as P

P_SIZE = 32
WIN = 256
LAGS = 128
REACH = 1000


HIGHEST = lax.Precision.HIGHEST


def with_halo(block, sides, width):
    for axis, dim in sides:
        count = lax.axis_size(axis)
        forward = [(i, i + 1) for i in range(count - 1)]
        backward = [(target, source) for source, target in forward]
        low = lax.ppermute(
            lax.slice_in_dim(block, block.shape[dim] - width, None, axis=dim), axis, forward
        )
        high = lax.ppermute(lax.slice_in_dim(block, 0, width, axis=dim), axis, backward)
        block = jnp.concatenate([low, block, high], axis=dim)
    return block


def from_root(value, axis, source):
    kept = jnp.where(lax.axis_index(axis) == source, value, 0).astype(value.dtype)
    return lax.psum(kept, axis)


def fir_matrix(fir_taps):
    tap_count = fir_taps.shape[0]
    row_index = jnp.arange(2 * (tap_count - 1))[:, None]
    col_index = jnp.arange(tap_count - 1)[None, :]
    offset = row_index - col_index
    is_valid = (offset >= 0) & (offset < tap_count)
    picked = jnp.take(fir_taps.astype(jnp.float32), jnp.clip(offset, 0, tap_count - 1))
    return jnp.where(is_valid, picked, jnp.float32(0.0))


def spectral_table(window_len):
    quarter = window_len // 4
    sample = jnp.arange(window_len)[:, None]
    column = jnp.arange(window_len)[None, :]
    bin_number = column // (2 * quarter) * quarter + column % quarter
    part_flag = column // quarter % 2
    phase = jnp.mod(bin_number * sample, window_len).astype(jnp.float32) * jnp.float32(
        2.0 * math.pi / window_len
    )
    entries = jnp.where(part_flag == 0, jnp.cos(phase), -jnp.sin(phase)) / jnp.float32(
        math.sqrt(window_len)
    )
    return entries.astype(jnp.bfloat16)


def lag_matrix(first_half, halves, quarter, window_len, lag_count):
    column = jnp.arange(halves * 2 * quarter, dtype=jnp.int32)[:, None]
    bin_number = (first_half + column // (2 * quarter)) * quarter + column % quarter
    part_flag = column // quarter % 2
    lag_shift = jnp.arange(lag_count, dtype=jnp.int32)[None, :] - lag_count // 2
    phase = jnp.mod(bin_number * lag_shift, window_len).astype(jnp.float32) * jnp.float32(
        2.0 * math.pi / window_len
    )
    return jnp.where(part_flag == 0, jnp.cos(phase), -jnp.sin(phase))


def band_taper(band_edges, bin_count):
    bin_values = jnp.arange(bin_count).astype(jnp.float32)
    edges = band_edges.astype(jnp.float32)
    rising = 0.5 - 0.5 * jnp.cos(
        jnp.float32(math.pi) * (bin_values - edges[0]) / (edges[1] - edges[0])
    )
    falling = 0.5 - 0.5 * jnp.cos(
        jnp.float32(math.pi) * (edges[3] - bin_values) / (edges[3] - edges[2])
    )
    inner = jnp.where(bin_values < edges[3], falling, jnp.float32(0.0))
    inner = jnp.where(bin_values <= edges[2], jnp.float32(1.0), inner)
    inner = jnp.where(bin_values < edges[1], rising, inner)
    return jnp.where(bin_values <= edges[0], jnp.float32(0.0), inner)


def whiten(spectra, band_edges):
    window_len = spectra.shape[-1]
    quarter = window_len // 4
    bin_count = window_len // 2
    leading = spectra.shape[:-1]
    split = spectra.reshape(leading + (2, 2, quarter))
    power = (split[..., 0, :] * split[..., 0, :] + split[..., 1, :] * split[..., 1, :]).reshape(
        leading + (bin_count,)
    )
    mean_power = jnp.mean(power, axis=-2)
    bin_values = jnp.arange(bin_count)
    smoother = (jnp.abs(bin_values[:, None] - bin_values[None, :]) <= 4).astype(jnp.float32)
    counts = jnp.sum(smoother, axis=0)
    levels = jnp.dot(mean_power, smoother, precision=HIGHEST) / counts
    factor = band_taper(band_edges, bin_count) / jnp.sqrt(levels + 1e-06)
    factor = factor.reshape(factor.shape[:-1] + (2, 1, quarter))
    return (split * jnp.expand_dims(factor, -4)).astype(jnp.bfloat16)


def cross_terms(receiver_part, partner):
    recv_real = receiver_part[:, :, :, 0]
    recv_imag = receiver_part[:, :, :, 1]
    part_real = partner[:, :, :, 0]
    part_imag = partner[:, :, :, 1]
    real_sum = jnp.einsum(
        "rwhf,rwhf->rhf", recv_real, part_real, preferred_element_type=jnp.float32
    ) + jnp.einsum("rwhf,rwhf->rhf", recv_imag, part_imag, preferred_element_type=jnp.float32)
    imag_sum = jnp.einsum(
        "rwhf,rwhf->rhf", recv_imag, part_real, preferred_element_type=jnp.float32
    ) - jnp.einsum("rwhf,rwhf->rhf", recv_real, part_imag, preferred_element_type=jnp.float32)
    return jnp.stack([real_sum, imag_sum], axis=2).reshape(receiver_part.shape[0], -1)


def shards(raw, fir_taps, spatial_taps, band_edges, source_owner, source_panel, source_pick):
    channels, samples = raw.shape
    margin = (fir_taps.shape[0] - 1) // 2
    extended = with_halo(raw, ((("tm", "sub"), 1),), margin)
    blocks = extended.reshape(channels, samples // (2 * margin) + 1, 2 * margin)
    windows = jnp.concatenate([blocks[:, :-1], blocks[:, 1:]], axis=2)
    filtered = jnp.einsum(
        "cbi,ij->cbj",
        windows,
        fir_matrix(fir_taps).astype(jnp.bfloat16),
        preferred_element_type=jnp.float32,
    ).reshape(channels, samples)
    side_len = spatial_taps.shape[0] // 2
    bordered = with_halo(filtered, (("chan", 0),), side_len)
    shaped = jnp.zeros_like(filtered)
    for tap_index in range(spatial_taps.shape[0]):
        shaped = shaped + spatial_taps[tap_index] * bordered[tap_index : tap_index + channels]
    shaped = shaped.astype(jnp.bfloat16)
    window_len = WIN
    quarter = window_len // 4
    frames = shaped.reshape(channels, samples // window_len, window_len)
    spectra = jnp.einsum(
        "cwn,nk->cwk", frames, spectral_table(window_len), preferred_element_type=jnp.float32
    )
    whitened = whiten(spectra, band_edges)
    lag_table = lag_matrix(0, 2, quarter, window_len, LAGS)
    total_frames = samples // window_len * lax.axis_size("tm") * lax.axis_size("sub")
    norm_scale = 1.0 / math.sqrt(total_frames * (window_len // 2))
    receivers = lax.axis_index("chan") * channels + jnp.arange(channels, dtype=jnp.int32)
    panel_width = P_SIZE

    def one_step(state_in, inputs):
        owner_index, panel_index, pick_row = inputs
        own_panel = lax.dynamic_slice_in_dim(whitened, panel_index * panel_width, panel_width, 0)
        own_panel = own_panel.reshape(panel_width, -1)
        sources = from_root(own_panel, "chan", owner_index)
        selector = (pick_row[:, None] == jnp.arange(panel_width, dtype=jnp.int32)[None, :]).astype(
            jnp.bfloat16
        )
        partner = jnp.dot(selector, sources, preferred_element_type=jnp.float32).astype(
            jnp.bfloat16
        )
        partner = partner.reshape(whitened.shape)
        cross_sum = cross_terms(whitened, partner)
        lagged = jnp.dot(cross_sum, lag_table, precision=HIGHEST) * norm_scale
        distance = jnp.abs(
            receivers - (owner_index * channels + panel_index * panel_width + pick_row)
        )
        lagged = jnp.where((distance <= REACH)[:, None], lagged, jnp.float32(0.0))
        return (state_in, lagged)

    unused, stacked = lax.scan(
        one_step, jnp.zeros((), jnp.int32), (source_owner, source_panel, source_pick)
    )
    stacked = lax.psum(stacked, ("tm", "sub"))
    return stacked


def solution(mesh):
    placed = (
        P(("grp", "chan"), ("tm", "sub")),
        P(),
        P(),
        P(),
        P("grp"),
        P(),
        P(None, ("grp", "chan")),
    )
    return jax.shard_map(
        shards,
        mesh=mesh,
        in_specs=placed,
        out_specs=P(None, ("grp", "chan"), None),
        check_vma=False,
    )
```

profile of v0, /device:TPU:0, one launch (start us, length us, event | category | flops | bytes accessed | tf_op | source)
XLA Modules:
  0.0 773.0 jit_solution(6123850707603630516)
XLA Ops:
  7.4 1.7 copy.38
  9.0 1.3 collective-permute-start.1
  10.3 3.0 collective-permute-start
  14.9 191.6 %gather_fusion = bf16[32768]{0:T(1024)(128)(2,1)S(1)} fusion(bf16[129]{0:T(256)(128)(2,1)S(1)} %copy-done, s32[32768]{0:T(1024)S(1)} %fusion.79), kind=kCustom, calls=%fused_computation | custom fusion | bytes 262144 | tf_op jit(solution)/shard_map/jit(_take)/gather | solution.py:41
  210.9 0.7 fusion.60
  211.7 1.3 collective-permute-start.3
  213.0 5.8 collective-permute-start.2
  218.7 2.5 compare_select_fusion.9
  221.2 1.9 copy.43
  223.1 2.0 copy.45
  225.1 2.0 copy.44
  227.1 20.2 %fusion.41 = bf16[128,4096]{0,1:T(8,128)(2,1)S(1)} fusion(f32[128,4096]{0,1:T(8,128)S(1)} %bitcast.125, f32[4,4096]{0,1:T(8,128)} %copy.45, f32[4,4096]{0,1:T(8,128)} %copy.44, f32[]{:T(128)} %bitcast.23, f32[]{:T(128)} %bitcast.22, f32[]{:T(128)} %bitcast.21, f32[]{:T(128)} %bitcast.19, f32[]{:T(128)} %bitcast.18, f32[]{:T(128)} %bitcast.17, f32[]{:T(128)} %bitcast.16, ...), kind=kLoop, calls=%fused_computation.71 | loop fusion | flops 13631488 | bytes 3276836 | tf_op jit(solution)/shard_map/convert_element_type | solution.py:136
  247.3 1.5 fusion.76
  249.7 478.6 %while.13 = (s32[]{:T(128)}, f32[8,128,128]{2,1,0:T(8,128)}, s32[8]{0:T(128)S(1)}, s32[8]{0:T(128)S(1)}, s32[8,128]{1,0:T(8,128)}, /*index=5*/bf16[128,16,2,2,64...) while((s32[]{:T(128)}, f32[8,128,128]{2,1,0:T(8,128)}, ...), condition=%wide.region_4.5_spmd.clone, body=%wide.region_2.4_spmd.clone.sunk | while | flops 88380048 | bytes 10293089 | solution.py:170
  252.0 1.5 dynamic-slice_select_fusion.2
  254.9 51.3 %all-reduce.5.cloned.1.call-done = bf16[32,4096]{0,1:T(8,128)(2,1)} async-done(((bf16[32,4096]{0,1:T(8,128)(2,1)}), bf16[32,4096]{0,1:T(8,128)(2,1)}) %all-reduce.5.cloned.1.call-update) | async-done | bytes 262160 | tf_op jit(solution)/shard_map/while/body/eval_jaxpr/psum | solution.py:32
  306.2 1.7 convolution_convert_fusion.2
  309.0 1.5 fusion.145
  313.0 1.5 dynamic-slice_select_fusion.2
  315.8 50.0 %all-reduce.5.cloned.1.call-done = bf16[32,4096]{0,1:T(8,128)(2,1)} async-done(((bf16[32,4096]{0,1:T(8,128)(2,1)}), bf16[32,4096]{0,1:T(8,128)(2,1)}) %all-reduce.5.cloned.1.call-update) | async-done | bytes 262160 | tf_op jit(solution)/shard_map/while/body/eval_jaxpr/psum | solution.py:32
  365.9 1.7 convolution_convert_fusion.2
  368.7 1.5 fusion.145
  372.6 1.5 dynamic-slice_select_fusion.2
  375.5 50.0 %all-reduce.5.cloned.1.call-done = bf16[32,4096]{0,1:T(8,128)(2,1)} async-done(((bf16[32,4096]{0,1:T(8,128)(2,1)}), bf16[32,4096]{0,1:T(8,128)(2,1)}) %all-reduce.5.cloned.1.call-update) | async-done | bytes 262160 | tf_op jit(solution)/shard_map/while/body/eval_jaxpr/psum | solution.py:32
  425.5 1.7 convolution_convert_fusion.2
  428.4 1.5 fusion.145
  432.3 1.5 dynamic-slice_select_fusion.2
  435.1 50.0 %all-reduce.5.cloned.1.call-done = bf16[32,4096]{0,1:T(8,128)(2,1)} async-done(((bf16[32,4096]{0,1:T(8,128)(2,1)}), bf16[32,4096]{0,1:T(8,128)(2,1)}) %all-reduce.5.cloned.1.call-update) | async-done | bytes 262160 | tf_op jit(solution)/shard_map/while/body/eval_jaxpr/psum | solution.py:32
  485.2 1.7 convolution_convert_fusion.2
  488.0 1.6 fusion.145
  492.0 1.5 dynamic-slice_select_fusion.2
  494.8 50.0 %all-reduce.5.cloned.1.call-done = bf16[32,4096]{0,1:T(8,128)(2,1)} async-done(((bf16[32,4096]{0,1:T(8,128)(2,1)}), bf16[32,4096]{0,1:T(8,128)(2,1)}) %all-reduce.5.cloned.1.call-update) | async-done | bytes 262160 | tf_op jit(solution)/shard_map/while/body/eval_jaxpr/psum | solution.py:32
  544.8 1.7 convolution_convert_fusion.2
  547.7 1.5 fusion.145
  551.6 1.5 dynamic-slice_select_fusion.2
  554.5 50.0 %all-reduce.5.cloned.1.call-done = bf16[32,4096]{0,1:T(8,128)(2,1)} async-done(((bf16[32,4096]{0,1:T(8,128)(2,1)}), bf16[32,4096]{0,1:T(8,128)(2,1)}) %all-reduce.5.cloned.1.call-update) | async-done | bytes 262160 | tf_op jit(solution)/shard_map/while/body/eval_jaxpr/psum | solution.py:32
  604.5 1.7 convolution_convert_fusion.2
  607.4 1.5 fusion.145
  611.3 1.5 dynamic-slice_select_fusion.2
  614.1 50.0 %all-reduce.5.cloned.1.call-done = bf16[32,4096]{0,1:T(8,128)(2,1)} async-done(((bf16[32,4096]{0,1:T(8,128)(2,1)}), bf16[32,4096]{0,1:T(8,128)(2,1)}) %all-reduce.5.cloned.1.call-update) | async-done | bytes 262160 | tf_op jit(solution)/shard_map/while/body/eval_jaxpr/psum | solution.py:32
  664.2 1.7 convolution_convert_fusion.2
  667.0 1.5 fusion.145
  670.9 1.5 dynamic-slice_select_fusion.2
  673.8 50.0 %all-reduce.5.cloned.1.call-done = bf16[32,4096]{0,1:T(8,128)(2,1)} async-done(((bf16[32,4096]{0,1:T(8,128)(2,1)}), bf16[32,4096]{0,1:T(8,128)(2,1)}) %all-reduce.5.cloned.1.call-update) | async-done | bytes 262160 | tf_op jit(solution)/shard_map/while/body/eval_jaxpr/psum | solution.py:32
  723.8 1.7 convolution_convert_fusion.2
  726.7 1.5 fusion.145
  728.8 34.9 %all-reduce.3.cloned.1.call-done = f32[8,128,128]{2,1,0:T(8,128)} async-done(((f32[8,128,128]{2,1,0:T(8,128)}), f32[8,128,128]{2,1,0:T(8,128)}) %all-reduce.3.cloned.1.call-update) | async-done | bytes 524304 | tf_op jit(solution)/shard_map/psum | solution.py:173
  763.7 1.9 copy.91
  (111 shorter events, 28.9 us)
Async XLA Ops:
  7.4 7.5 copy-start
  7.4 6.1 copy-start.2
  7.4 6.8 copy-start.3
  9.0 199.9 %collective-permute-start.1 = (bf16[128,64]{0,1:T(8,128)(2,1)S(1)}, bf16[128,64]{0,1:T(8,128)(2,1)S(1)}, u32[]{:S(2)}, u32[]{:S(2)}) collective-permute-start(bf16[128,64]{0,1:T(8,128)(2,1)S(1)} %get-tuple-element.177), channel_id=1, source_target_pairs={{1,0},{2,1},{3,2},{5,4},{6,5},{7,6},{9,8},{10,9},{11,10},{13,12},{... | collective-permute-start | bytes 49160 | tf_op jit(solution)/shard_map/ppermute | solution.py:25
  10.3 198.6 %collective-permute-start = (bf16[128,64]{0,1:T(8,128)(2,1)S(1)}, bf16[128,64]{0,1:T(8,128)(2,1)S(1)}, u32[]{:S(2)}, u32[]{:S(2)}) collective-permute-start(bf16[128,64]{0,1:T(8,128)(2,1)S(1)} %get-tuple-element.176), channel_id=1, source_target_pairs={{0,1},{1,2},{2,3},{4,5},{5,6},{6,7},{8,9},{9,10},{10,11},{12,13},{... | collective-permute-start | bytes 49160 | tf_op jit(solution)/shard_map/ppermute | solution.py:22
  211.6 7.1 copy-start.1
  211.7 11.5 %collective-permute-start.3 = (f32[4,4096]{1,0:T(4,128)S(1)}, f32[4,4096]{1,0:T(4,128)S(1)}, u32[]{:S(2)}, u32[]{:S(2)}) collective-permute-start(f32[4,4096]{1,0:T(4,128)S(1)} %get-tuple-element.173), channel_id=1, source_target_pairs={{4,0},{8,4},{12,8},{5,1},{9,5},{13,9},{6,2},{10,6},{14,10},{7,3},{... | collective-permute-start | bytes 196616 | tf_op jit(solution)/shard_map/ppermute | solution.py:25
  213.0 12.2 %collective-permute-start.2 = (f32[4,4096]{1,0:T(4,128)S(1)}, f32[4,4096]{1,0:T(4,128)S(1)}, u32[]{:S(2)}, u32[]{:S(2)}) collective-permute-start(f32[4,4096]{1,0:T(4,128)S(1)} %get-tuple-element.172), channel_id=1, source_target_pairs={{0,4},{4,8},{8,12},{1,5},{5,9},{9,13},{2,6},{6,10},{10,14},{3,7},{... | collective-permute-start | bytes 196616 | tf_op jit(solution)/shard_map/ppermute | solution.py:22
  249.0 0.7 copy-start.4
  249.0 0.7 copy-start.5
  249.7 56.5 %all-reduce.5.cloned.1.call-start = ((), (), s32[]{:S(2)}) async-start(), calls=%async_computation.1 | async-start | bytes 2097152 | tf_op jit(solution)/shard_map/while/body/eval_jaxpr/psum | solution.py:32
  310.6 55.3 %all-reduce.5.cloned.1.call-start = ((), (), s32[]{:S(2)}) async-start(), calls=%async_computation.1 | async-start | bytes 2097152 | tf_op jit(solution)/shard_map/while/body/eval_jaxpr/psum | solution.py:32
  370.3 55.3 %all-reduce.5.cloned.1.call-start = ((), (), s32[]{:S(2)}) async-start(), calls=%async_computation.1 | async-start | bytes 2097152 | tf_op jit(solution)/shard_map/while/body/eval_jaxpr/psum | solution.py:32
  429.9 55.3 %all-reduce.5.cloned.1.call-start = ((), (), s32[]{:S(2)}) async-start(), calls=%async_computation.1 | async-start | bytes 2097152 | tf_op jit(solution)/shard_map/while/body/eval_jaxpr/psum | solution.py:32
  489.6 55.3 %all-reduce.5.cloned.1.call-start = ((), (), s32[]{:S(2)}) async-start(), calls=%async_computation.1 | async-start | bytes 2097152 | tf_op jit(solution)/shard_map/while/body/eval_jaxpr/psum | solution.py:32
  549.2 55.3 %all-reduce.5.cloned.1.call-start = ((), (), s32[]{:S(2)}) async-start(), calls=%async_computation.1 | async-start | bytes 2097152 | tf_op jit(solution)/shard_map/while/body/eval_jaxpr/psum | solution.py:32
  608.9 55.3 %all-reduce.5.cloned.1.call-start = ((), (), s32[]{:S(2)}) async-start(), calls=%async_computation.1 | async-start | bytes 2097152 | tf_op jit(solution)/shard_map/while/body/eval_jaxpr/psum | solution.py:32
  668.6 55.3 %all-reduce.5.cloned.1.call-start = ((), (), s32[]{:S(2)}) async-start(), calls=%async_computation.1 | async-start | bytes 2097152 | tf_op jit(solution)/shard_map/while/body/eval_jaxpr/psum | solution.py:32
  728.2 35.4 %all-reduce.3.cloned.1.call-start = ((), (), s32[]{:S(2)}) async-start(), calls=%async_computation | async-start | bytes 1048576 | tf_op jit(solution)/shard_map/psum | solution.py:173
Sparse Core Ops, SparseCore 0:
  253.7 52.4 all-reduce.4
  314.6 51.1 all-reduce.4
  374.3 51.1 all-reduce.4
  433.9 51.2 all-reduce.4
  493.6 51.1 all-reduce.4
  553.3 51.2 all-reduce.4
  612.9 51.1 all-reduce.4
  672.6 51.1 all-reduce.4
Sparse Core Ops, SparseCore 1:
  731.0 32.6 all-reduce.2
where the time goes:
time: 774 us; the launch traced here: 773 us
  waiting for transfers between devices  437 us (56%)
  local copies, waits for them, and re-layouts  219 us (28%)
  other arithmetic  44.6 us (6%)
  matrix products  28.5 us (4%)
  between operations  17.5 us (2%)
  loops' own time  15 us (2%)
  starting transfers between devices  11.4 us (1%)
    psum x8, waiting for transfers between devices, from_root(): return lax.psum(kept, axis)  402 us
    gather x1, local copies, waits for them, and re-layouts, fir_matrix(): jnp.take(fir_taps.astype(jnp.float32), jnp.clip(offset, 0, tap_count - 1))  192 us
    psum x1, waiting for transfers between devices, shards(): stacked = lax.psum(stacked, ('tm', 'sub'))  34.9 us
    convert_element_type x1, other arithmetic, shards(): shaped = shaped.astype(jnp.bfloat16)  20.2 us
  transfers between devices with their start and end apart: 13, of which 9 were waited for; matrix products, arithmetic and copies ran while one was open for 27% of the time, Pallas kernels for 0%

commit v1 on v0

v1 whole, which is shorter than its diff:
```python
import functools
import math

import jax
import jax.numpy as jnp
import numpy as np
from jax import lax
from jax.experimental import pallas as pl
from jax.experimental.pallas import tpu as pltpu
from jax.sharding import PartitionSpec as P

P_SIZE = 32
WIN = 256
LAGS = 128
REACH = 1000
HIGHEST = lax.Precision.HIGHEST


def column_maps():
    column = np.arange(WIN)
    quarter = WIN // 4
    bins = column // (2 * quarter) * quarter + column % quarter
    parts = column // quarter % 2
    return bins, parts


def spectral_table():
    bins, parts = column_maps()
    angle = 2.0 * np.pi * ((bins[None, :] * np.arange(WIN)[:, None]) % WIN) / WIN
    table = np.where(parts == 0, np.cos(angle), -np.sin(angle)) / math.sqrt(WIN)
    return jnp.asarray(table.astype(np.float32)).astype(jnp.bfloat16)


def smooth_table():
    bins, _ = column_maps()
    near = np.abs(bins[:, None] - bins[None, :]) <= 4
    return jnp.asarray(near.astype(np.float32)), near.sum(0).astype(np.float32)[None, :] / 2.0


def lag_tables(scale):
    bins, parts = column_maps()
    lag = np.arange(LAGS) - LAGS // 2
    angle = 2.0 * np.pi * ((bins[:, None] * lag[None, :]) % WIN) / WIN
    real = np.cos(angle) * scale
    imag = np.where(parts[:, None] == 0, -np.sin(angle), np.sin(angle)) * scale
    return jnp.asarray(real.astype(np.float32)), jnp.asarray(imag.astype(np.float32))


def shift_perm(count, step):
    return [(i, i + step) for i in range(count) if 0 <= i + step < count]


def taper_row(edges_ref):
    column = lax.broadcasted_iota(jnp.int32, (1, WIN), 1)
    quarter = WIN // 4
    bins = (column // (2 * quarter) * quarter + column % quarter).astype(jnp.float32)
    e0, e1, e2, e3 = [jnp.full((1, WIN), edges_ref[k]).astype(jnp.float32) for k in range(4)]
    rising = 0.5 - 0.5 * jnp.cos(math.pi * (bins - e0) / (e1 - e0))
    falling = 0.5 - 0.5 * jnp.cos(math.pi * (e3 - bins) / (e3 - e2))
    inner = jnp.where(bins < e3, falling, 0.0)
    inner = jnp.where(bins <= e2, 1.0, inner)
    inner = jnp.where(bins < e1, rising, inner)
    return jnp.where(bins <= e0, 0.0, inner)


def white_kernel(frames, channels, side, taps_ref, sp_ref, edges_ref, ext_ref, table_ref, near_ref,
                 count_ref, out_ref, filt, spec):
    depth = taps_ref.shape[1]
    rolled = pltpu.roll(jnp.broadcast_to(taps_ref[...], (WIN, depth)), 0, 1, stride=1, stride_axis=0)
    fir_t = rolled.astype(jnp.bfloat16)
    power = jnp.zeros((channels, WIN), jnp.float32)
    for w in range(frames):
        block = ext_ref[:, w * WIN : w * WIN + depth]
        got = lax.dot_general(block, fir_t, (((1,), (1,)), ((), ())), preferred_element_type=jnp.float32)
        slot = w % 2
        filt[slot, 8 : 8 + channels] = got[:channels]
        filt[slot, 8 - side : 8] = got[channels : channels + side]
        filt[slot, 8 + channels : 8 + channels + side] = got[channels + side : channels + 2 * side]
        shaped = sp_ref[0] * filt[slot, 8 - side : 8 - side + channels]
        for m in range(1, 2 * side + 1):
            shaped += sp_ref[m] * filt[slot, 8 - side + m : 8 - side + m + channels]
        spectra = jnp.dot(shaped.astype(jnp.bfloat16), table_ref[...], preferred_element_type=jnp.float32)
        spec[w] = spectra
        power += spectra * spectra
    level = jnp.dot(power, near_ref[...], precision=HIGHEST, preferred_element_type=jnp.float32)
    level = level / (count_ref[...] * frames)
    factor = taper_row(edges_ref) / jnp.sqrt(level + 1e-06)
    for w in range(frames):
        out_ref[w] = (spec[w] * factor).astype(jnp.bfloat16)


def cross_kernel(frames, channels, start_ref, pick_ref, white_ref, panel_ref, real_ref, imag_ref,
                 base_ref, out_ref, plain, swapped):
    step = pl.program_id(0)
    half = WIN // 2

    @pl.when(step == 0)
    def _():
        for w in range(frames):
            value = white_ref[w].astype(jnp.float32)
            plain[w] = value
            for h in range(2):
                swapped[w, :, h * half : (h + 1) * half] = pltpu.roll(
                    value[:, h * half : (h + 1) * half], half // 2, 1
                )

    rows = channels // 2
    start = start_ref[step]
    for r in range(2):
        here = slice(r * rows, (r + 1) * rows)
        pick = pick_ref[0, here]
        chosen = (pick == lax.broadcasted_iota(jnp.int32, (rows, P_SIZE), 1)).astype(jnp.bfloat16)
        acc_p = jnp.zeros((rows, WIN), jnp.float32)
        acc_q = jnp.zeros((rows, WIN), jnp.float32)
        for w in range(frames):
            partner = jnp.dot(chosen, panel_ref[0, w], preferred_element_type=jnp.float32)
            acc_p += plain[w, here] * partner
            acc_q += swapped[w, here] * partner
        lagged = jnp.dot(acc_p, real_ref[...], precision=HIGHEST, preferred_element_type=jnp.float32)
        lagged += jnp.dot(acc_q, imag_ref[...], precision=HIGHEST, preferred_element_type=jnp.float32)
        receiver = base_ref[0] + r * rows + lax.broadcasted_iota(jnp.int32, (rows, 1), 0)
        far = jnp.abs(receiver - (start + pick)) > REACH
        out_ref[0, here] = jnp.where(far, 0.0, lagged)


SMEM = pl.BlockSpec(memory_space=pltpu.SMEM)
VMEM = pl.BlockSpec(memory_space=pltpu.VMEM)


def shards(raw, fir_taps, spatial_taps, band_edges, source_owner, source_panel, source_pick):
    channels, samples = raw.shape
    margin = (fir_taps.shape[0] - 1) // 2
    side = spatial_taps.shape[0] // 2
    frames = samples // WIN
    steps = source_owner.shape[0]
    times = ("tm", "sub")
    count = lax.axis_size(times)
    low = lax.ppermute(raw[:, samples - margin :], times, shift_perm(count, 1))
    high = lax.ppermute(raw[:, :margin], times, shift_perm(count, -1))
    ext = jnp.concatenate([low, raw, high], axis=1)
    n_chan = lax.axis_size("chan")
    below = lax.ppermute(ext[channels - side :], "chan", shift_perm(n_chan, 1))
    above = lax.ppermute(ext[:side], "chan", shift_perm(n_chan, -1))
    spare = jnp.zeros((16 - 2 * side, ext.shape[1]), ext.dtype)
    ext = jnp.concatenate([ext, below, above, spare], axis=0)
    depth = WIN + 2 * margin
    taps = jnp.pad(fir_taps.astype(jnp.float32), (0, depth - fir_taps.shape[0]))[None, :]
    near, counts = smooth_table()
    white = pl.pallas_call(
        functools.partial(white_kernel, frames, channels, side),
        out_shape=jax.ShapeDtypeStruct((frames, channels, WIN), jnp.bfloat16),
        in_specs=[VMEM, SMEM, SMEM, VMEM, VMEM, VMEM, VMEM],
        out_specs=VMEM,
        scratch_shapes=[
            pltpu.VMEM((2, channels + 16, WIN), jnp.float32),
            pltpu.VMEM((frames, channels, WIN), jnp.float32),
        ],
        compiler_params=pltpu.CompilerParams(vmem_limit_bytes=32 * 2**20),
        name="white",
    )(taps, spatial_taps, band_edges, ext, spectral_table(), near, jnp.asarray(counts))

    me = lax.axis_index("chan")
    own = jnp.stack([
        jnp.where(
            source_owner[s] == me,
            lax.dynamic_slice_in_dim(white, source_panel[s] * P_SIZE, P_SIZE, 1),
            jnp.zeros((), white.dtype),
        )
        for s in range(steps)
    ])
    panels = lax.psum(own, "chan")

    total = frames * count
    real, imag = lag_tables(1.0 / math.sqrt(total * (WIN // 2)))
    start = source_owner * channels + source_panel * P_SIZE
    base = (me * channels)[None]
    lagged = pl.pallas_call(
        functools.partial(cross_kernel, frames, channels),
        grid=(steps,),
        out_shape=jax.ShapeDtypeStruct((steps, channels, LAGS), jnp.float32),
        in_specs=[
            SMEM,
            pl.BlockSpec((1, channels, 1), lambda s: (s, 0, 0)),
            pl.BlockSpec((frames, channels, WIN), lambda s: (0, 0, 0)),
            pl.BlockSpec((1, frames, P_SIZE, WIN), lambda s: (s, 0, 0, 0)),
            pl.BlockSpec((WIN, LAGS), lambda s: (0, 0)),
            pl.BlockSpec((WIN, LAGS), lambda s: (0, 0)),
            SMEM,
        ],
        out_specs=pl.BlockSpec((1, channels, LAGS), lambda s: (s, 0, 0)),
        scratch_shapes=[pltpu.VMEM((frames, channels, WIN), jnp.float32)] * 2,
        compiler_params=pltpu.CompilerParams(vmem_limit_bytes=32 * 2**20),
        name="cross",
    )(start, source_pick[:, :, None], white, panels, real, imag, base)
    return lax.psum(lagged, times)


def solution(mesh):
    placed = (
        P(("grp", "chan"), ("tm", "sub")),
        P(),
        P(),
        P(),
        P("grp"),
        P(),
        P(None, ("grp", "chan")),
    )
    return jax.shard_map(
        shards,
        mesh=mesh,
        in_specs=placed,
        out_specs=P(None, ("grp", "chan"), None),
        check_vma=False,
    )
```

time: 774 us -> 189 us (0.24)
  waiting for transfers between devices: 437 us -> 124 us
  local copies, waits for them, and re-layouts: 219 us -> 10.8 us
  other arithmetic: 44.6 us -> 6.37 us
  matrix products: 28.5 us -> 0 us
  Pallas kernels: 0 us -> 15.1 us
  loops' own time: 15 us -> 0 us
    psum x9 -> x2, waiting for transfers between devices: 436 us -> 124 us  [the longest x1 91.2 us: shards(): panels = lax.psum(own, 'chan')]
    gather x1 -> x0, local copies, waits for them, and re-layouts: 192 us -> none  [fir_matrix(): jnp.take(fir_taps.astype(jnp.float32), jnp.clip(offset, 0, tap_count - 1))]
    dot_general x19 -> x0, matrix products: 28.5 us -> none  [the longest x8 13.6 us: one_step(): jnp.dot(selector, sources, preferred_element_type=jnp.float32)]
    convert_element_type x3 -> x0, other arithmetic: 20.5 us -> none  [the longest x1 20.2 us: shards(): shaped = shaped.astype(jnp.bfloat16)]
    pallas_call x0 -> x2, Pallas kernels: none -> 15.1 us  [the longest x1 9.82 us: shards(): pl.pallas_call(functools.partial(cross_kernel, frames, channels), grid=(s...]
    another operation x1 -> x0, loops' own time: 15 us -> none  [shards(): lax.scan(one_step, jnp.zeros((), jnp.int32), (source_owner, source_panel,...]
    select_n x9 -> x0, other arithmetic: 14.4 us -> none  [the longest x8 11.9 us: from_root(): jnp.where(lax.axis_index(axis) == source, value, 0).astype(value.dtype)]
    dynamic_slice x16 -> x0, local copies, waits for them, and re-layouts: 9.36 us -> none  [shards(): lax.scan(one_step, jnp.zeros((), jnp.int32), (source_owner, source_panel,...]
  transfers between devices with their start and end apart: 13 -> 6, of which waited for: 9 -> 3; matrix products, arithmetic and copies ran while one was open for 27% -> 2% of each run, Pallas kernels for 0% -> 0%
where the time goes in v1:
time: 189 us
  waiting for transfers between devices  124 us (66%)
  between operations  23.7 us (13%)
  Pallas kernels  15.1 us (8%)
  local copies, waits for them, and re-layouts  10.8 us (6%)
  starting transfers between devices  8.82 us (5%)
  other arithmetic  6.37 us (3%)
    psum x1, waiting for transfers between devices, shards(): panels = lax.psum(own, 'chan')  91.2 us
    psum x1, waiting for transfers between devices, shards(): return lax.psum(lagged, times)  32.3 us
    pallas_call x1, Pallas kernels, shards(): pl.pallas_call(functools.partial(cross_kernel, frames, channels), grid=(s...  9.82 us
    unnamed x7, other arithmetic  5.32 us
    pallas_call x1, Pallas kernels, shards(): pl.pallas_call(functools.partial(white_kernel, frames, channels, side), o...  5.29 us
    ppermute x1, starting transfers between devices, shards(): below = lax.ppermute(ext[channels - side:], 'chan', shift_perm(n_chan, 1))  3.84 us
  transfers between devices with their start and end apart: 6, of which 3 were waited for; matrix products, arithmetic and copies ran while one was open for 2% of the time, Pallas kernels for 0%

profile of v1, /device:TPU:0, one launch (start us, length us, event | category | flops | bytes accessed | tf_op | source)
XLA Modules:
  0.0 188.9 jit_solution(9086213877196176910)
XLA Ops:
  6.5 0.0 all-reduce.4.cloned.1.call-start
  6.5 0.9 fusion.1
  7.4 2.3 %collective-permute-start = (bf16[128,64]{1,0:T(8,128)(2,1)S(1)}, bf16[128,64]{1,0:T(8,128)(2,1)S(1)}, u32[]{:S(2)}, u32[]{:S(2)}) collective-permute-start(bf16[128,64]{1,0:T(8,128)(2,1)S(1)} %get-tuple-element.8), channel_id=1, source_target_pairs={{0,1},{1,2},{2,3},{4,5},{5,6},{6,7},{8,9},{9,10},{10,11},{12,13},{... | collective-permute-start | bytes 49160 | tf_op jit(solution)/shard_map/ppermute | solution.py:138
  9.8 1.3 collective-permute-start.1
  11.1 1.6 fusion.3
  12.7 1.6 fusion.2
  14.3 0.0 copy-start.4
  14.3 0.0 copy-start.5
  14.3 0.0 copy-start.6
  14.4 0.0 copy-start.7
  14.4 0.0 collective-permute-done
  14.4 0.6 collective-permute-done.1
  15.0 2.9 %concatenate.6 = bf16[128,4224]{1,0:T(8,128)(2,1)S(1)} concatenate(bf16[128,64]{1,0:T(8,128)(2,1)S(1)} %collective-permute-done, bf16[128,4096]{1,0:T(8,128)(2,1)} %param.12, bf16[128,64]{1,0:T(8,128)(2,1)S(1)} %collective-permute-done.1), dimensions={1} | concatenate | bytes 2162688 | tf_op jit(solution)/shard_map/concatenate | solution.py:140
  17.9 3.8 %collective-permute-start.2 = (bf16[4,4224]{1,0:T(4,128)(2,1)S(1)}, bf16[4,4224]{1,0:T(4,128)(2,1)S(1)}, u32[]{:S(2)}, u32[]{:S(2)}) collective-permute-start(bf16[4,4224]{1,0:T(4,128)(2,1)S(1)} %get-tuple-element.5), channel_id=1, source_target_pairs={{0,4},{4,8},{8,12},{1,5},{5,9},{9,13},{2,6},{6,10},{10,14},{3,7},{... | collective-permute-start | bytes 101384 | tf_op jit(solution)/shard_map/ppermute | solution.py:142
  21.7 1.3 collective-permute-start.3
  23.0 0.0 copy-done.11
  33.1 0.1 pad.9.clone
  33.2 0.0 collective-permute-done.2
  33.2 0.0 collective-permute-done.3
  33.2 0.3 maximum_maximum_fusion.ext_ref
  33.5 0.0 copy-done.1
  33.5 0.0 copy-done.4
  33.5 0.0 copy-done.5
  33.5 0.0 copy-done.6
  33.5 0.0 copy-done.7
  33.5 5.3 %white.1.white_ref = bf16[16,128,256]{2,1,0:T(8,128)(2,1)S(1)} custom-call(f32[1,384]{1,0:T(1,128)S(1)} %reshape.16.taps_ref, f32[9]{0:T(128)S(1)} %copy-done.6, s32[4]{0:T(128)S(1)} %copy-done.7, bf16[144,4224]{1,0:T(8,128)(2,1)S(1)} %maximum_maximum_fusion.ext_ref, bf16[256,256]{1,0:T(8,128)(2,1)S(1)} %copy-done.4, f32[256,256]{1,0:T(8,128)S(1)} %copy-done.1, ...), custom_call_target="tpu_custom_call" | custom-call | tf_op jit(solution)/shard_map/white/pallas_call | solution.py:149
  38.8 0.8 bitcast_dynamic-update-slice_fusion.7
  39.6 0.8 bitcast_dynamic-update-slice_fusion.6
  40.3 0.8 bitcast_dynamic-update-slice_fusion.5
  41.1 0.8 bitcast_dynamic-update-slice_fusion.4
  41.9 0.8 bitcast_dynamic-update-slice_fusion.3
  42.6 0.8 bitcast_dynamic-update-slice_fusion.2
  43.4 0.8 bitcast_dynamic-update-slice_fusion.1
  44.2 0.8 bitcast_dynamic-update-slice_fusion
  44.9 0.0 all-reduce.4.cloned.1.call-update
  44.9 0.0 all-reduce.6.cloned.1.call-start
  45.0 0.0 copy-done.10
  45.0 0.2 copy.13.pick_ref
  45.2 0.0 copy-done.8
  45.2 0.0 copy-done.9
  45.3 91.2 %all-reduce.4.cloned.1.call-done.panel_ref = bf16[8,16,32,256]{3,2,1,0:T(8,128)(2,1)} async-done(((bf16[8,16,32,256]{3,2,1,0:T(8,128)(2,1)}), bf16[8,16,32,256]{3,2,1,0:T(8,128)(2,1)}) %all-reduce.4.cloned.1.call-update) | async-done | bytes 2097168 | tf_op jit(solution)/shard_map/psum | solution.py:171
  136.5 0.0 copy-done.2
  136.5 0.0 copy-done.3
  136.5 1.6 copy-done
  138.1 9.8 %cross.1 = f32[8,128,128]{2,1,0:T(8,128)} custom-call(s32[8]{0:T(128)S(1)} %multiply_add_fusion.start_ref, s32[8,128,1]{2,1,0:T(8,128)S(1)} %copy.13.pick_ref, bf16[16,128,256]{2,1,0:T(8,128)(2,1)S(1)} %white.1.white_ref, bf16[8,16,32,256]{3,2,1,0:T(8,128)(2,1)S(1)} %copy-done, f32[256,128]{1,0:T(8,128)S(1)} %copy-done.2, f32[256,128]{1,0:T(8,128)S(1)} %copy-done.3, ...), custom_call_target="tpu_custom_call" | custom-call | tf_op jit(solution)/shard_map/cross/pallas_call | solution.py:177
  147.9 0.0 all-reduce.6.cloned.1.call-update
  147.9 32.3 %all-reduce.6.cloned.1.call-done = f32[8,128,128]{2,1,0:T(8,128)} async-done(((f32[8,128,128]{2,1,0:T(8,128)}), f32[8,128,128]{2,1,0:T(8,128)}) %all-reduce.6.cloned.1.call-update) | async-done | bytes 524304 | tf_op jit(solution)/shard_map/psum | solution.py:195
  180.2 1.9 copy.23
  (13 shorter events, 0.1 us)
Async XLA Ops:
  6.5 16.5 %copy-start.11 = (bf16[129]{0:T(256)(128)(2,1)S(1)}, bf16[129]{0:T(256)(128)(2,1)}, u32[]{:S(2)}) copy-start(bf16[129]{0:T(256)(128)(2,1)} %param.13) | copy-start | bytes 778
  6.5 129.9 %all-reduce.4.cloned.1.call-start = ((), (), s32[]{:S(2)}) async-start(), calls=%async_computation | async-start | bytes 4194304 | tf_op jit(solution)/shard_map/psum | solution.py:171
  7.4 7.0 %collective-permute-start = (bf16[128,64]{1,0:T(8,128)(2,1)S(1)}, bf16[128,64]{1,0:T(8,128)(2,1)S(1)}, u32[]{:S(2)}, u32[]{:S(2)}) collective-permute-start(bf16[128,64]{1,0:T(8,128)(2,1)S(1)} %get-tuple-element.8), channel_id=1, source_target_pairs={{0,1},{1,2},{2,3},{4,5},{5,6},{6,7},{8,9},{9,10},{10,11},{12,13},{... | collective-permute-start | bytes 49160 | tf_op jit(solution)/shard_map/ppermute | solution.py:138
  9.8 5.2 %collective-permute-start.1 = (bf16[128,64]{1,0:T(8,128)(2,1)S(1)}, bf16[128,64]{1,0:T(8,128)(2,1)S(1)}, u32[]{:S(2)}, u32[]{:S(2)}) collective-permute-start(bf16[128,64]{1,0:T(8,128)(2,1)S(1)} %get-tuple-element.7), channel_id=1, source_target_pairs={{1,0},{2,1},{3,2},{5,4},{6,5},{7,6},{9,8},{10,9},{11,10},{13,12},{... | collective-permute-start | bytes 49160 | tf_op jit(solution)/shard_map/ppermute | solution.py:139
  14.3 19.2 %copy-start.1 = (f32[256,256]{1,0:T(8,128)S(1)}, f32[256,256]{1,0:T(8,128)}, u32[]{:S(2)}) copy-start(f32[256,256]{1,0:T(8,128)} %constant.37.clone.near_ref) | copy-start | bytes 786436
  14.3 19.2 %copy-start.4 = (bf16[256,256]{1,0:T(8,128)(2,1)S(1)}, bf16[256,256]{1,0:T(8,128)(2,1)}, u32[]{:S(2)}) copy-start(bf16[256,256]{1,0:T(8,128)(2,1)} %constant.44.table_ref) | copy-start | bytes 393220
  14.3 19.2 %copy-start.5 = (f32[1,256]{1,0:T(1,128)S(1)}, f32[1,256]{1,0:T(1,128)}, u32[]{:S(2)}) copy-start(f32[1,256]{1,0:T(1,128)} %constant.39.clone.count_ref) | copy-start | bytes 3076
  14.3 19.2 %copy-start.6 = (f32[9]{0:T(128)S(1)}, f32[9]{0:T(128)}, u32[]{:S(2)}) copy-start(f32[9]{0:T(128)} %sp_ref.1) | copy-start | bytes 112
  14.4 19.2 %copy-start.7 = (s32[4]{0:T(128)S(1)}, s32[4]{0:T(128)}, u32[]{:S(2)}) copy-start(s32[4]{0:T(128)} %edges_ref.1) | copy-start | bytes 52
  17.9 15.3 %collective-permute-start.2 = (bf16[4,4224]{1,0:T(4,128)(2,1)S(1)}, bf16[4,4224]{1,0:T(4,128)(2,1)S(1)}, u32[]{:S(2)}, u32[]{:S(2)}) collective-permute-start(bf16[4,4224]{1,0:T(4,128)(2,1)S(1)} %get-tuple-element.5), channel_id=1, source_target_pairs={{0,4},{4,8},{8,12},{1,5},{5,9},{9,13},{2,6},{6,10},{10,14},{3,7},{... | collective-permute-start | bytes 101384 | tf_op jit(solution)/shard_map/ppermute | solution.py:142
  21.7 11.5 %collective-permute-start.3 = (bf16[4,4224]{1,0:T(4,128)(2,1)S(1)}, bf16[4,4224]{1,0:T(4,128)(2,1)S(1)}, u32[]{:S(2)}, u32[]{:S(2)}) collective-permute-start(bf16[4,4224]{1,0:T(4,128)(2,1)S(1)} %get-tuple-element.6), channel_id=1, source_target_pairs={{4,0},{8,4},{12,8},{5,1},{9,5},{13,9},{6,2},{10,6},{14,10},{7,3},{... | collective-permute-start | bytes 101384 | tf_op jit(solution)/shard_map/ppermute | solution.py:143
  41.9 3.1 %copy-start.10 = (s32[8,128]{1,0:T(8,128)S(1)}, s32[8,128]{1,0:T(8,128)}, u32[]{:S(2)}) copy-start(s32[8,128]{1,0:T(8,128)} %param.18) | copy-start | bytes 12292
  42.6 2.6 %copy-start.8 = (s32[8]{0:T(128)S(1)}, s32[8]{0:T(128)}, u32[]{:S(2)}) copy-start(s32[8]{0:T(128)} %param.17) | copy-start | bytes 100
  42.6 2.6 %copy-start.9 = (s32[8]{0:T(128)S(1)}, s32[8]{0:T(128)}, u32[]{:S(2)}) copy-start(s32[8]{0:T(128)} %param.16) | copy-start | bytes 100
  42.6 93.8 %copy-start.2 = (f32[256,128]{1,0:T(8,128)S(1)}, f32[256,128]{1,0:T(8,128)}, u32[]{:S(2)}) copy-start(f32[256,128]{1,0:T(8,128)} %constant.40.clone.real_ref) | copy-start | bytes 393220
  42.6 93.8 %copy-start.3 = (f32[256,128]{1,0:T(8,128)S(1)}, f32[256,128]{1,0:T(8,128)}, u32[]{:S(2)}) copy-start(f32[256,128]{1,0:T(8,128)} %constant.41.clone.imag_ref) | copy-start | bytes 393220
  44.9 135.3 %all-reduce.6.cloned.1.call-start = ((), (), s32[]{:S(2)}) async-start(), calls=%async_computation.1 | async-start | bytes 1048576 | tf_op jit(solution)/shard_map/psum | solution.py:195
  136.5 1.6 copy-start
Sparse Core Ops, SparseCore 0:
  45.1 91.3 all-reduce.3
  148.0 32.1 all-reduce.5

commit v2 on v1

--- a/solution.py
+++ b/solution.py
@@ -63,8 +63,8 @@
     return jnp.where(bins <= e0, 0.0, inner)
 
 
-def white_kernel(frames, channels, side, taps_ref, sp_ref, edges_ref, ext_ref, table_ref, near_ref,
-                 count_ref, out_ref, filt, spec):
+def white_kernel(frames, channels, side, steps, taps_ref, sp_ref, edges_ref, panel_ref, ext_ref, table_ref,
+                 near_ref, count_ref, out_ref, own_ref, filt, spec):
     depth = taps_ref.shape[1]
     rolled = pltpu.roll(jnp.broadcast_to(taps_ref[...], (WIN, depth)), 0, 1, stride=1, stride_axis=0)
     fir_t = rolled.astype(jnp.bfloat16)
@@ -87,40 +87,204 @@
     factor = taper_row(edges_ref) / jnp.sqrt(level + 1e-06)
     for w in range(frames):
         out_ref[w] = (spec[w] * factor).astype(jnp.bfloat16)
-
-
-def cross_kernel(frames, channels, start_ref, pick_ref, white_ref, panel_ref, real_ref, imag_ref,
-                 base_ref, out_ref, plain, swapped):
-    step = pl.program_id(0)
+    for s in range(steps):
+        first = pl.multiple_of(panel_ref[s] * P_SIZE, P_SIZE)
+        for w in range(frames):
+            own_ref[s, w] = out_ref[w, pl.ds(first, P_SIZE)]
+
+
+SPLIT = 4
+LAG = 2
+MESH = pl.DeviceIdType.MESH
+
+
+def cross_kernel(frames, channels, steps, n_chan, n_tm, n_sub, owner_ref, panel_ref, pick_ref, white_ref, own_ref,
+                 real_ref, imag_ref, out_ref, plain, swapped, in_low, in_high, to_high, to_low, own_lag,
+                 sub_in, tm_in, done, sem_high, sem_low, got_low, got_high, sub_send, sub_recv,
+                 tm_send, tm_recv, fin_send, fin_recv):
+    me = lax.axis_index("chan")
+    my_tm = lax.axis_index("tm")
+    my_sub = lax.axis_index("sub")
     half = WIN // 2
-
-    @pl.when(step == 0)
+    part = channels // n_sub
+    group = frames // SPLIT
+    chunks = steps * SPLIT
+
+    barrier = pltpu.get_barrier_semaphore()
+    peers = [{"chan": lax.rem(me + d, n_chan)} for d in (1, n_chan - 1)]
+    peers += [{"tm": lax.rem(my_tm + d, n_tm)} for d in range(1, n_tm)]
+    peers += [{"sub": lax.rem(my_sub + d, n_sub)} for d in range(1, n_sub)]
+    for peer in peers:
+        pl.semaphore_signal(barrier, inc=1, device_id=peer, device_id_type=MESH)
+    pl.semaphore_wait(barrier, len(peers))
+
+    def up(c):
+        return pltpu.make_async_remote_copy(
+            src_ref=to_high.at[c], dst_ref=in_low.at[c], send_sem=sem_high.at[c], recv_sem=got_low.at[c],
+            device_id={"chan": lax.rem(me + 1, n_chan)}, device_id_type=MESH)
+
+    def down(c):
+        return pltpu.make_async_remote_copy(
+            src_ref=to_low.at[c], dst_ref=in_high.at[c], send_sem=sem_low.at[c], recv_sem=got_high.at[c],
+            device_id={"chan": lax.rem(me + n_chan - 1, n_chan)}, device_id_type=MESH)
+
+    def sub_copy(s, d):
+        to = lax.rem(my_sub + d, n_sub)
+        return pltpu.make_async_remote_copy(
+            src_ref=own_lag.at[s, pl.ds(to * part, part)], dst_ref=sub_in.at[s, d - 1],
+            send_sem=sub_send.at[s, d - 1], recv_sem=sub_recv.at[s, d - 1],
+            device_id={"sub": to}, device_id_type=MESH)
+
+    def tm_copy(s, d):
+        return pltpu.make_async_remote_copy(
+            src_ref=tm_in.at[s, my_tm], dst_ref=tm_in.at[s, my_tm],
+            send_sem=tm_send.at[s, d - 1], recv_sem=tm_recv.at[s, d - 1],
+            device_id={"tm": lax.rem(my_tm + d, n_tm)}, device_id_type=MESH)
+
+    def fin_copy(s, d):
+        here = pl.ds(my_sub * part, part)
+        return pltpu.make_async_remote_copy(
+            src_ref=done.at[s, here], dst_ref=done.at[s, here],
+            send_sem=fin_send.at[s, d - 1], recv_sem=fin_recv.at[s, d - 1],
+            device_id={"sub": lax.rem(my_sub + d, n_sub)}, device_id_type=MESH)
+
+    @pl.when(me == 0)
     def _():
-        for w in range(frames):
-            value = white_ref[w].astype(jnp.float32)
-            plain[w] = value
-            for h in range(2):
-                swapped[w, :, h * half : (h + 1) * half] = pltpu.roll(
-                    value[:, h * half : (h + 1) * half], half // 2, 1
-                )
-
-    rows = channels // 2
-    start = start_ref[step]
-    for r in range(2):
-        here = slice(r * rows, (r + 1) * rows)
-        pick = pick_ref[0, here]
-        chosen = (pick == lax.broadcasted_iota(jnp.int32, (rows, P_SIZE), 1)).astype(jnp.bfloat16)
-        acc_p = jnp.zeros((rows, WIN), jnp.float32)
-        acc_q = jnp.zeros((rows, WIN), jnp.float32)
-        for w in range(frames):
-            partner = jnp.dot(chosen, panel_ref[0, w], preferred_element_type=jnp.float32)
-            acc_p += plain[w, here] * partner
-            acc_q += swapped[w, here] * partner
-        lagged = jnp.dot(acc_p, real_ref[...], precision=HIGHEST, preferred_element_type=jnp.float32)
-        lagged += jnp.dot(acc_q, imag_ref[...], precision=HIGHEST, preferred_element_type=jnp.float32)
-        receiver = base_ref[0] + r * rows + lax.broadcasted_iota(jnp.int32, (rows, 1), 0)
-        far = jnp.abs(receiver - (start + pick)) > REACH
-        out_ref[0, here] = jnp.where(far, 0.0, lagged)
+        in_low[...] = jnp.zeros_like(in_low)
+
+    @pl.when(me == n_chan - 1)
+    def _():
+        in_high[...] = jnp.zeros_like(in_high)
+
+    def stage(c, arrived, leaving):
+        s = lax.div(c, SPLIT)
+        k = lax.rem(c, SPLIT)
+        mine = jnp.full((P_SIZE, WIN), owner_ref[s], jnp.int32) == me
+        for w in range(group):
+            leaving[c, w] = jnp.where(mine, own_ref[s, k * group + w], arrived[c, w])
+
+    def relay(t):
+        c = t - LAG * me
+
+        @pl.when((c >= 0) & (c < chunks))
+        def _():
+            @pl.when(me > 0)
+            def _():
+                up(c).wait_recv()
+
+            @pl.when(me < n_chan - 1)
+            def _():
+                stage(c, in_low, to_high)
+                up(c).start()
+
+        e = t - LAG * (n_chan - 1 - me)
+
+        @pl.when((e >= 0) & (e < chunks))
+        def _():
+            @pl.when(me < n_chan - 1)
+            def _():
+                down(e).wait_recv()
+
+            @pl.when(me > 0)
+            def _():
+                stage(e, in_high, to_low)
+                down(e).start()
+
+    def compute(s):
+        rows = channels // 2
+        owner = owner_ref[s]
+        where = jnp.full((P_SIZE, WIN), owner, jnp.int32)
+        start = owner * channels + panel_ref[s] * P_SIZE
+        chosen = []
+        for r in range(2):
+            pick = pick_ref[s, r * rows : (r + 1) * rows]
+            chosen.append((pick == lax.broadcasted_iota(jnp.int32, (rows, P_SIZE), 1)).astype(jnp.bfloat16))
+        for r in range(2):
+            here = slice(r * rows, (r + 1) * rows)
+            acc_p = jnp.zeros((rows, WIN), jnp.float32)
+            acc_q = jnp.zeros((rows, WIN), jnp.float32)
+            for w in range(frames):
+                c = s * SPLIT + w // group
+                value = jnp.where(where < me, in_low[c, w % group], in_high[c, w % group])
+                value = jnp.where(where == me, own_ref[s, w], value)
+                partner = jnp.dot(chosen[r], value, preferred_element_type=jnp.float32)
+                acc_p += plain[w, here] * partner
+                acc_q += swapped[w, here] * partner
+            lagged = jnp.dot(acc_p, real_ref[...], precision=HIGHEST, preferred_element_type=jnp.float32)
+            lagged += jnp.dot(acc_q, imag_ref[...], precision=HIGHEST, preferred_element_type=jnp.float32)
+            receiver = me * channels + r * rows + lax.broadcasted_iota(jnp.int32, (rows, 1), 0)
+            far = jnp.abs(receiver - (start + pick_ref[s, here])) > REACH
+            own_lag[s, here] = jnp.where(far, 0.0, lagged)
+        for d in range(1, n_sub):
+            sub_copy(s, d).start()
+
+    def sub_sum(s):
+        total = own_lag[s, pl.ds(my_sub * part, part)]
+        for d in range(1, n_sub):
+            sub_copy(s, d).wait_recv()
+            total += sub_in[s, d - 1]
+        tm_in[s, my_tm] = total
+        for d in range(1, n_tm):
+            tm_copy(s, d).start()
+
+    def tm_sum(s):
+        for d in range(1, n_tm):
+            tm_copy(s, d).wait_recv()
+        total = tm_in[s, 0]
+        for k in range(1, n_tm):
+            total += tm_in[s, k]
+        done[s, pl.ds(my_sub * part, part)] = total
+        for d in range(1, n_sub):
+            fin_copy(s, d).start()
+
+    def finish(s):
+        for d in range(1, n_sub):
+            fin_copy(s, d).wait_recv()
+        out_ref[s] = done[s]
+
+    delay = -(-(n_chan - 1) * LAG // SPLIT)
+
+    def turn(u, carry):
+        for k in range(SPLIT):
+            relay(u * SPLIT + k)
+
+        @pl.when(u == 0)
+        def _():
+            for w in range(frames):
+                value = white_ref[w].astype(jnp.float32)
+                plain[w] = value
+                for h in range(2):
+                    swapped[w, :, h * half : (h + 1) * half] = pltpu.roll(
+                        value[:, h * half : (h + 1) * half], half // 2, 1)
+
+        for late, work in enumerate((compute, sub_sum, tm_sum, finish)):
+            s = u - delay - late
+            pl.when((s >= 0) & (s < steps))(functools.partial(work, s))
+        return carry
+
+    lax.fori_loop(0, steps + delay + 3, turn, 0)
+
+    def drain_chunk(c, carry):
+        @pl.when(me < n_chan - 1)
+        def _():
+            up(c).wait_send()
+
+        @pl.when(me > 0)
+        def _():
+            down(c).wait_send()
+        return carry
+
+    lax.fori_loop(0, chunks, drain_chunk, 0)
+
+    def drain_step(s, carry):
+        for d in range(1, n_sub):
+            sub_copy(s, d).wait_send()
+            fin_copy(s, d).wait_send()
+        for d in range(1, n_tm):
+            tm_copy(s, d).wait_send()
+        return carry
+
+    lax.fori_loop(0, steps, drain_step, 0)
 
 
 SMEM = pl.BlockSpec(memory_space=pltpu.SMEM)
@@ -146,53 +310,51 @@
     depth = WIN + 2 * margin
     taps = jnp.pad(fir_taps.astype(jnp.float32), (0, depth - fir_taps.shape[0]))[None, :]
     near, counts = smooth_table()
-    white = pl.pallas_call(
-        functools.partial(white_kernel, frames, channels, side),
-        out_shape=jax.ShapeDtypeStruct((frames, channels, WIN), jnp.bfloat16),
-        in_specs=[VMEM, SMEM, SMEM, VMEM, VMEM, VMEM, VMEM],
-        out_specs=VMEM,
+    white, own = pl.pallas_call(
+        functools.partial(white_kernel, frames, channels, side, steps),
+        out_shape=[
+            jax.ShapeDtypeStruct((frames, channels, WIN), jnp.bfloat16),
+            jax.ShapeDtypeStruct((steps, frames, P_SIZE, WIN), jnp.bfloat16),
+        ],
+        in_specs=[VMEM, SMEM, SMEM, SMEM, VMEM, VMEM, VMEM, VMEM],
+        out_specs=[VMEM, VMEM],
         scratch_shapes=[
             pltpu.VMEM((2, channels + 16, WIN), jnp.float32),
             pltpu.VMEM((frames, channels, WIN), jnp.float32),
         ],
         compiler_params=pltpu.CompilerParams(vmem_limit_bytes=32 * 2**20),
         name="white",
-    )(taps, spatial_taps, band_edges, ext, spectral_table(), near, jnp.asarray(counts))
-
-    me = lax.axis_index("chan")
-    own = jnp.stack([
-        jnp.where(
-            source_owner[s] == me,
-            lax.dynamic_slice_in_dim(white, source_panel[s] * P_SIZE, P_SIZE, 1),
-            jnp.zeros((), white.dtype),
-        )
-        for s in range(steps)
-    ])
-    panels = lax.psum(own, "chan")
+    )(taps, spatial_taps, band_edges, source_panel, ext, spectral_table(), near, jnp.asarray(counts))
 
     total = frames * count
     real, imag = lag_tables(1.0 / math.sqrt(total * (WIN // 2)))
-    start = source_owner * channels + source_panel * P_SIZE
-    base = (me * channels)[None]
-    lagged = pl.pallas_call(
-        functools.partial(cross_kernel, frames, channels),
-        grid=(steps,),
+    n_tm, n_sub = lax.axis_size("tm"), lax.axis_size("sub")
+    chunks = steps * SPLIT
+    flow = pltpu.VMEM((chunks, frames // SPLIT, P_SIZE, WIN), jnp.bfloat16)
+    part = channels // n_sub
+    dma = pltpu.SemaphoreType.DMA
+    return pl.pallas_call(
+        functools.partial(cross_kernel, frames, channels, steps, n_chan, n_tm, n_sub),
         out_shape=jax.ShapeDtypeStruct((steps, channels, LAGS), jnp.float32),
-        in_specs=[
-            SMEM,
-            pl.BlockSpec((1, channels, 1), lambda s: (s, 0, 0)),
-            pl.BlockSpec((frames, channels, WIN), lambda s: (0, 0, 0)),
-            pl.BlockSpec((1, frames, P_SIZE, WIN), lambda s: (s, 0, 0, 0)),
-            pl.BlockSpec((WIN, LAGS), lambda s: (0, 0)),
-            pl.BlockSpec((WIN, LAGS), lambda s: (0, 0)),
-            SMEM,
+        in_specs=[SMEM, SMEM, VMEM, VMEM, VMEM, VMEM, VMEM],
+        out_specs=VMEM,
+        scratch_shapes=[
+            pltpu.VMEM((frames, channels, WIN), jnp.float32),
+            pltpu.VMEM((frames, channels, WIN), jnp.float32),
+            flow, flow, flow, flow,
+            pltpu.VMEM((steps, channels, LAGS), jnp.float32),
+            pltpu.VMEM((steps, n_sub - 1, part, LAGS), jnp.float32),
+            pltpu.VMEM((steps, n_tm, part, LAGS), jnp.float32),
+            pltpu.VMEM((steps, channels, LAGS), jnp.float32),
+            dma((chunks,)), dma((chunks,)), dma((chunks,)), dma((chunks,)),
+            dma((steps, n_sub - 1)), dma((steps, n_sub - 1)),
+            dma((steps, n_tm - 1)), dma((steps, n_tm - 1)),
+            dma((steps, n_sub - 1)), dma((steps, n_sub - 1)),
         ],
-        out_specs=pl.BlockSpec((1, channels, LAGS), lambda s: (s, 0, 0)),
-        scratch_shapes=[pltpu.VMEM((frames, channels, WIN), jnp.float32)] * 2,
-        compiler_params=pltpu.CompilerParams(vmem_limit_bytes=32 * 2**20),
+        compiler_params=pltpu.CompilerParams(
+            vmem_limit_bytes=40 * 2**20, collective_id=0, has_side_effects=True),
         name="cross",
-    )(start, source_pick[:, :, None], white, panels, real, imag, base)
-    return lax.psum(lagged, times)
+    )(source_owner, source_panel, source_pick[:, :, None], white, own, real, imag)
 
 
 def solution(mesh):

time: 189 us -> 103 us (0.54)
  waiting for transfers between devices: 124 us -> 7.99 us
  Pallas kernels: 15.1 us -> 80.5 us
  between operations: 23.7 us -> 0.27 us
  other arithmetic: 6.37 us -> 0.29 us
  local copies, waits for them, and re-layouts: 10.8 us -> 4.93 us
    psum x2 -> x0, waiting for transfers between devices: 124 us -> none  [the longest x1 91.2 us: shards(): panels = lax.psum(own, 'chan')]
    pallas_call x2, Pallas kernels: 15.1 us -> 80.5 us  [the longest x1 75.1 us: shards(): pl.pallas_call(functools.partial(cross_kernel, frames, channels, steps, n...]
    unnamed x7 -> x0, other arithmetic: 5.32 us -> none
    ppermute x1, waiting for transfers between devices: 0.01 us -> 4.08 us  [shards(): above = lax.ppermute(ext[:side], 'chan', shift_perm(n_chan, -1))]
    ppermute x1, waiting for transfers between devices: 0.59 us -> 3.9 us  [shards(): high = lax.ppermute(raw[:, :margin], times, shift_perm(count, -1))]
    slice x2 -> x0, local copies, waits for them, and re-layouts: 3.25 us -> none  [the longest x1 1.63 us: shards(): source_owner[s] == me]
    unnamed x25 -> x23, local copies, waits for them, and re-layouts: 3.51 us -> 0.86 us
  transfers between devices with their start and end apart: 6 -> 4, of which waited for: 3 -> 2; matrix products, arithmetic and copies ran while one was open for 2% -> 0% of each run, Pallas kernels for 0% -> 0%
where the time goes in v2:
time: 103 us; the launch traced here: 102 us
  Pallas kernels  80.5 us (78%)
  starting transfers between devices  8.42 us (8%)
  waiting for transfers between devices  7.99 us (8%)
  local copies, waits for them, and re-layouts  4.93 us (5%)
    pallas_call x1, Pallas kernels, shards(): pl.pallas_call(functools.partial(cross_kernel, frames, channels, steps, n...  75.1 us
    pallas_call x1, Pallas kernels, shards(): pl.pallas_call(functools.partial(white_kernel, frames, channels, side, st...  5.44 us
    ppermute x1, waiting for transfers between devices, shards(): above = lax.ppermute(ext[:side], 'chan', shift_perm(n_chan, -1))  4.08 us
    ppermute x1, waiting for transfers between devices, shards(): high = lax.ppermute(raw[:, :margin], times, shift_perm(count, -1))  3.9 us
    ppermute x1, starting transfers between devices, shards(): below = lax.ppermute(ext[channels - side:], 'chan', shift_perm(n_chan, 1))  3.48 us
    concatenate x1, local copies, waits for them, and re-layouts, shards(): ext = jnp.concatenate([low, raw, high], axis=1)  2.85 us
    ppermute x1, starting transfers between devices, shards(): low = lax.ppermute(raw[:, samples - margin:], times, shift_perm(count, 1))  2.35 us
  transfers between devices with their start and end apart: 4, of which 2 were waited for; matrix products, arithmetic and copies ran while one was open for 0% of the time, Pallas kernels for 0%

profile of v2, /device:TPU:0, one launch (start us, length us, event | category | flops | bytes accessed | tf_op | source)
XLA Modules:
  0.0 102.4 jit_solution(15640342599335173906)
XLA Ops:
  0.0 0.0 copy-start.10
  0.0 0.0 copy-start.9
  0.0 0.9 fusion.1
  0.9 2.3 %collective-permute-start = (bf16[128,64]{1,0:T(8,128)(2,1)S(1)}, bf16[128,64]{1,0:T(8,128)(2,1)S(1)}, u32[]{:S(2)}, u32[]{:S(2)}) collective-permute-start(bf16[128,64]{1,0:T(8,128)(2,1)S(1)} %get-tuple-element.12), channel_id=1, source_target_pairs={{0,1},{1,2},{2,3},{4,5},{5,6},{6,7},{8,9},{9,10},{10,11},{12,13},{... | collective-permute-start | bytes 49160 | tf_op jit(solution)/shard_map/ppermute | solution.py:302
  3.2 1.3 %collective-permute-start.1 = (bf16[128,64]{1,0:T(8,128)(2,1)S(1)}, bf16[128,64]{1,0:T(8,128)(2,1)S(1)}, u32[]{:S(2)}, u32[]{:S(2)}) collective-permute-start(bf16[128,64]{1,0:T(8,128)(2,1)S(1)} %get-tuple-element.11), channel_id=1, source_target_pairs={{1,0},{2,1},{3,2},{5,4},{6,5},{7,6},{9,8},{10,9},{11,10},{13,12},{... | collective-permute-start | bytes 49160 | tf_op jit(solution)/shard_map/ppermute | solution.py:303
  4.5 0.0 collective-permute-done
  4.6 3.9 %collective-permute-done.1 = bf16[128,64]{1,0:T(8,128)(2,1)S(1)} collective-permute-done((bf16[128,64]{1,0:T(8,128)(2,1)S(1)}, bf16[128,64]{1,0:T(8,128)(2,1)S(1)}, u32[]{:S(2)}, u32[]{:S(2)}) %collective-permute-start.1) | collective-permute-done | bytes 16416 | tf_op jit(solution)/shard_map/ppermute | solution.py:303
  8.4 2.9 %concatenate.6 = bf16[128,4224]{1,0:T(8,128)(2,1)S(1)} concatenate(bf16[128,64]{1,0:T(8,128)(2,1)S(1)} %collective-permute-done, bf16[128,4096]{1,0:T(8,128)(2,1)} %param.12, bf16[128,64]{1,0:T(8,128)(2,1)S(1)} %collective-permute-done.1), dimensions={1} | concatenate | bytes 2162688 | tf_op jit(solution)/shard_map/concatenate | solution.py:304
  11.3 3.5 %collective-permute-start.2 = (bf16[4,4224]{1,0:T(4,128)(2,1)S(1)}, bf16[4,4224]{1,0:T(4,128)(2,1)S(1)}, u32[]{:S(2)}, u32[]{:S(2)}) collective-permute-start(bf16[4,4224]{1,0:T(4,128)(2,1)S(1)} %get-tuple-element.9), channel_id=1, source_target_pairs={{0,4},{4,8},{8,12},{1,5},{5,9},{9,13},{2,6},{6,10},{10,14},{3,7},{... | collective-permute-start | bytes 101384 | tf_op jit(solution)/shard_map/ppermute | solution.py:306
  14.8 1.3 %collective-permute-start.3 = (bf16[4,4224]{1,0:T(4,128)(2,1)S(1)}, bf16[4,4224]{1,0:T(4,128)(2,1)S(1)}, u32[]{:S(2)}, u32[]{:S(2)}) collective-permute-start(bf16[4,4224]{1,0:T(4,128)(2,1)S(1)} %get-tuple-element.10), channel_id=1, source_target_pairs={{4,0},{8,4},{12,8},{5,1},{9,5},{13,9},{6,2},{10,6},{14,10},{7,3},{... | collective-permute-start | bytes 101384 | tf_op jit(solution)/shard_map/ppermute | solution.py:307
  16.1 0.0 copy-done.10
  16.2 0.0 copy-done.9
  16.2 0.2 copy.13.pick_ref
  16.4 0.0 copy-start
  16.4 0.0 copy-start.3
  16.4 0.0 copy-start.4
  16.4 0.0 copy-start.5
  16.5 0.0 copy-start.6
  16.5 0.0 copy-start.7
  16.5 0.1 pad.9.clone
  16.6 0.0 collective-permute-done.2
  16.6 4.1 %collective-permute-done.3 = bf16[4,4224]{1,0:T(4,128)(2,1)S(1)} collective-permute-done((bf16[4,4224]{1,0:T(4,128)(2,1)S(1)}, bf16[4,4224]{1,0:T(4,128)(2,1)S(1)}, u32[]{:S(2)}, u32[]{:S(2)}) %collective-permute-start.3) | collective-permute-done | bytes 33824 | tf_op jit(solution)/shard_map/ppermute | solution.py:307
  20.7 0.3 maximum_maximum_fusion.ext_ref
  20.9 0.0 copy-done
  21.0 0.0 copy-done.3
  21.0 0.0 copy-done.4
  21.0 0.0 copy-done.5
  21.0 0.0 copy-done.6
  21.0 0.0 copy-done.7
  21.0 0.0 copy-start.1
  21.0 0.0 copy-start.2
  21.0 0.0 copy-start.8
  21.0 5.4 %white.1 = (bf16[16,128,256]{2,1,0:T(8,128)(2,1)S(1)}, bf16[8,16,32,256]{3,2,1,0:T(8,128)(2,1)S(1)}) custom-call(f32[1,384]{1,0:T(1,128)S(1)} %reshape.taps_ref, f32[9]{0:T(128)S(1)} %copy-done.6, s32[4]{0:T(128)S(1)} %copy-done.7, s32[8]{0:T(128)S(1)} %copy-done.4, bf16[144,4224]{1,0:T(8,128)(2,1)S(1)} %maximum_maximum_fusion.ext_ref, ...), custom_call_target="tpu_custom_call" | custom-call | tf_op jit(solution)/shard_map/white/pallas_call | solution.py:313
  26.5 0.0 copy-done.1
  26.5 0.0 copy-done.2
  26.5 0.0 copy-done.8
  26.5 75.1 %cross.1 = f32[8,128,128]{2,1,0:T(8,128)S(1)} custom-call(s32[8]{0:T(128)S(1)} %copy-done.8, s32[8]{0:T(128)S(1)} %copy-done.4, s32[8,128,1]{2,1,0:T(8,128)S(1)} %copy.13.pick_ref, bf16[16,128,256]{2,1,0:T(8,128)(2,1)S(1)} %get-tuple-element.7.white_ref, bf16[8,16,32,256]{3,2,1,0:T(8,128)(2,1)S(1)} %get-tuple-element.8.own_ref, f32[256,128]{1,0:T(8,128)S(1)} %copy-done.1, ...), custom_call_target="tpu_custom_call" | custom-call | tf_op jit(solution)/shard_map/cross/pallas_call | solution.py:336
  101.6 0.8 copy.15
  (4 shorter events, 0.0 us)
Async XLA Ops:
  0.0 16.1 %copy-start.10 = (bf16[129]{0:T(256)(128)(2,1)S(1)}, bf16[129]{0:T(256)(128)(2,1)}, u32[]{:S(2)}) copy-start(bf16[129]{0:T(256)(128)(2,1)} %param.13) | copy-start | bytes 778
  0.0 16.2 %copy-start.9 = (s32[8,128]{1,0:T(8,128)S(1)}, s32[8,128]{1,0:T(8,128)}, u32[]{:S(2)}) copy-start(s32[8,128]{1,0:T(8,128)} %param.18) | copy-start | bytes 12292
  0.9 3.7 %collective-permute-start = (bf16[128,64]{1,0:T(8,128)(2,1)S(1)}, bf16[128,64]{1,0:T(8,128)(2,1)S(1)}, u32[]{:S(2)}, u32[]{:S(2)}) collective-permute-start(bf16[128,64]{1,0:T(8,128)(2,1)S(1)} %get-tuple-element.12), channel_id=1, source_target_pairs={{0,1},{1,2},{2,3},{4,5},{5,6},{6,7},{8,9},{9,10},{10,11},{12,13},{... | collective-permute-start | bytes 49160 | tf_op jit(solution)/shard_map/ppermute | solution.py:302
  3.2 5.2 %collective-permute-start.1 = (bf16[128,64]{1,0:T(8,128)(2,1)S(1)}, bf16[128,64]{1,0:T(8,128)(2,1)S(1)}, u32[]{:S(2)}, u32[]{:S(2)}) collective-permute-start(bf16[128,64]{1,0:T(8,128)(2,1)S(1)} %get-tuple-element.11), channel_id=1, source_target_pairs={{1,0},{2,1},{3,2},{5,4},{6,5},{7,6},{9,8},{10,9},{11,10},{13,12},{... | collective-permute-start | bytes 49160 | tf_op jit(solution)/shard_map/ppermute | solution.py:303
  11.3 5.2 %collective-permute-start.2 = (bf16[4,4224]{1,0:T(4,128)(2,1)S(1)}, bf16[4,4224]{1,0:T(4,128)(2,1)S(1)}, u32[]{:S(2)}, u32[]{:S(2)}) collective-permute-start(bf16[4,4224]{1,0:T(4,128)(2,1)S(1)} %get-tuple-element.9), channel_id=1, source_target_pairs={{0,4},{4,8},{8,12},{1,5},{5,9},{9,13},{2,6},{6,10},{10,14},{3,7},{... | collective-permute-start | bytes 101384 | tf_op jit(solution)/shard_map/ppermute | solution.py:306
  14.8 5.8 %collective-permute-start.3 = (bf16[4,4224]{1,0:T(4,128)(2,1)S(1)}, bf16[4,4224]{1,0:T(4,128)(2,1)S(1)}, u32[]{:S(2)}, u32[]{:S(2)}) collective-permute-start(bf16[4,4224]{1,0:T(4,128)(2,1)S(1)} %get-tuple-element.10), channel_id=1, source_target_pairs={{4,0},{8,4},{12,8},{5,1},{9,5},{13,9},{6,2},{10,6},{14,10},{7,3},{... | collective-permute-start | bytes 101384 | tf_op jit(solution)/shard_map/ppermute | solution.py:307
  16.4 4.5 %copy-start = (f32[256,256]{1,0:T(8,128)S(1)}, f32[256,256]{1,0:T(8,128)}, u32[]{:S(2)}) copy-start(f32[256,256]{1,0:T(8,128)} %constant.15.clone.near_ref) | copy-start | bytes 786436
  16.4 4.5 %copy-start.3 = (bf16[256,256]{1,0:T(8,128)(2,1)S(1)}, bf16[256,256]{1,0:T(8,128)(2,1)}, u32[]{:S(2)}) copy-start(bf16[256,256]{1,0:T(8,128)(2,1)} %constant.22.table_ref) | copy-start | bytes 393220
  16.4 4.5 %copy-start.4 = (s32[8]{0:T(128)S(1)}, s32[8]{0:T(128)}, u32[]{:S(2)}) copy-start(s32[8]{0:T(128)} %panel_ref.3) | copy-start | bytes 100
  16.4 4.5 %copy-start.5 = (f32[1,256]{1,0:T(1,128)S(1)}, f32[1,256]{1,0:T(1,128)}, u32[]{:S(2)}) copy-start(f32[1,256]{1,0:T(1,128)} %constant.17.clone.count_ref) | copy-start | bytes 3076
  16.5 4.5 %copy-start.6 = (f32[9]{0:T(128)S(1)}, f32[9]{0:T(128)}, u32[]{:S(2)}) copy-start(f32[9]{0:T(128)} %sp_ref.1) | copy-start | bytes 112
  16.5 4.5 %copy-start.7 = (s32[4]{0:T(128)S(1)}, s32[4]{0:T(128)}, u32[]{:S(2)}) copy-start(s32[4]{0:T(128)} %edges_ref.1) | copy-start | bytes 52
  21.0 5.5 %copy-start.1 = (f32[256,128]{1,0:T(8,128)S(1)}, f32[256,128]{1,0:T(8,128)}, u32[]{:S(2)}) copy-start(f32[256,128]{1,0:T(8,128)} %constant.18.clone.real_ref) | copy-start | bytes 393220
  21.0 5.5 %copy-start.2 = (f32[256,128]{1,0:T(8,128)S(1)}, f32[256,128]{1,0:T(8,128)}, u32[]{:S(2)}) copy-start(f32[256,128]{1,0:T(8,128)} %constant.19.clone.imag_ref) | copy-start | bytes 393220
  21.0 5.5 %copy-start.8 = (s32[8]{0:T(128)S(1)}, s32[8]{0:T(128)}, u32[]{:S(2)}) copy-start(s32[8]{0:T(128)} %owner_ref.1) | copy-start | bytes 100

commit v3 on v2

--- a/solution.py
+++ b/solution.py
@@ -63,14 +63,82 @@
     return jnp.where(bins <= e0, 0.0, inner)
 
 
-def white_kernel(frames, channels, side, steps, taps_ref, sp_ref, edges_ref, panel_ref, ext_ref, table_ref,
-                 near_ref, count_ref, out_ref, own_ref, filt, spec):
+LANES = 128
+MESH = pl.DeviceIdType.MESH
+
+
+def white_kernel(frames, channels, side, steps, n_chan, n_tm, n_sub, taps_ref, sp_ref, edges_ref, panel_ref,
+                 raw_ref, table_ref, near_ref, count_ref, out_ref, own_ref, filt, spec, ext, time_in,
+                 chan_out, chan_in, corner_out, corner_in, send_sem, recv_sem):
+    me = lax.axis_index("chan")
+    n_time = n_tm * n_sub
+    now = lax.axis_index("tm") * n_sub + lax.axis_index("sub")
+    samples = frames * WIN
     depth = taps_ref.shape[1]
+
+    def peer(dc, dt):
+        at = lax.rem(now + dt + n_time, n_time)
+        return {"chan": lax.rem(me + dc + n_chan, n_chan), "tm": lax.div(at, n_sub), "sub": lax.rem(at, n_sub)}
+
+    moves = [(0, 1), (0, -1), (1, 0), (-1, 0), (1, 1), (1, -1), (-1, 1), (-1, -1)]
+    barrier = pltpu.get_barrier_semaphore()
+    for dc, dt in moves:
+        pl.semaphore_signal(barrier, inc=1, device_id=peer(dc, dt), device_id_type=MESH)
+
+    ends = (slice(channels - side, channels), slice(0, side))
+    sides = (slice(samples - LANES, samples), slice(0, LANES))
+    for k in range(2):
+        chan_out[k] = raw_ref[ends[k]]
+        for h in range(2):
+            corner_out[2 * k + h] = raw_ref[ends[k], sides[h]]
+
+    def exists(dc, dt):
+        return (me + dc >= 0) & (me + dc < n_chan) & (now + dt >= 0) & (now + dt < n_time)
+
+    def copy(k):
+        dc, dt = moves[k]
+        if k < 2:
+            src, dst = raw_ref.at[:, sides[k]], time_in.at[k]
+        elif k < 4:
+            src, dst = chan_out.at[k - 2], chan_in.at[k - 2]
+        else:
+            src, dst = corner_out.at[k - 4], corner_in.at[k - 4]
+        return pltpu.make_async_remote_copy(
+            src_ref=src, dst_ref=dst, send_sem=send_sem.at[k], recv_sem=recv_sem.at[k],
+            device_id=peer(dc, dt), device_id_type=MESH)
+
+    pl.semaphore_wait(barrier, len(moves))
+    for k in (2, 3, 0, 1, 4, 5, 6, 7):
+        pl.when(exists(*moves[k]))(lambda k=k: copy(k).start())
+
+    ext[:channels, LANES : LANES + samples] = raw_ref[...]
     rolled = pltpu.roll(jnp.broadcast_to(taps_ref[...], (WIN, depth)), 0, 1, stride=1, stride_axis=0)
     fir_t = rolled.astype(jnp.bfloat16)
+
+    for k, (dc, dt) in enumerate(moves):
+        there = exists(-dc, -dt)
+        pl.when(there)(lambda k=k: copy(k).wait_recv())
+        buf, slot = (time_in, k) if k < 2 else (chan_in, k - 2) if k < 4 else (corner_in, k - 4)
+
+        @pl.when(jnp.logical_not(there))
+        def _():
+            buf[slot] = jnp.zeros(buf.shape[1:], buf.dtype)
+
+    def rows(low, high):
+        width = low.shape[1]
+        spare = jnp.zeros((16 - 2 * side, width), jnp.float32)
+        both = [low.astype(jnp.float32), high.astype(jnp.float32), spare]
+        return jnp.concatenate(both, axis=0).astype(jnp.bfloat16)
+
+    high_at = LANES + samples
+    ext[:channels, :LANES] = time_in[0]
+    ext[:channels, high_at:] = time_in[1]
+    ext[channels:, LANES:high_at] = rows(chan_in[0], chan_in[1])
+    ext[channels:, :LANES] = rows(corner_in[0], corner_in[2])
+    ext[channels:, high_at:] = rows(corner_in[1], corner_in[3])
     power = jnp.zeros((channels, WIN), jnp.float32)
     for w in range(frames):
-        block = ext_ref[:, w * WIN : w * WIN + depth]
+        block = ext[:, w * WIN : w * WIN + depth]
         got = lax.dot_general(block, fir_t, (((1,), (1,)), ((), ())), preferred_element_type=jnp.float32)
         slot = w % 2
         filt[slot, 8 : 8 + channels] = got[:channels]
@@ -88,14 +156,18 @@
     for w in range(frames):
         out_ref[w] = (spec[w] * factor).astype(jnp.bfloat16)
     for s in range(steps):
-        first = pl.multiple_of(panel_ref[s] * P_SIZE, P_SIZE)
+        panel = jnp.full((P_SIZE, WIN), panel_ref[s], jnp.int32)
         for w in range(frames):
-            own_ref[s, w] = out_ref[w, pl.ds(first, P_SIZE)]
+            value = out_ref[w, :P_SIZE]
+            for k in range(1, channels // P_SIZE):
+                value = jnp.where(panel == k, out_ref[w, k * P_SIZE : (k + 1) * P_SIZE], value)
+            own_ref[s, w] = value
+    for k, move in enumerate(moves):
+        pl.when(exists(*move))(lambda k=k: copy(k).wait_send())
 
 
 SPLIT = 4
-LAG = 2
-MESH = pl.DeviceIdType.MESH
+LAG = 3
 
 
 def cross_kernel(frames, channels, steps, n_chan, n_tm, n_sub, owner_ref, panel_ref, pick_ref, white_ref, own_ref,
@@ -299,19 +371,14 @@
     steps = source_owner.shape[0]
     times = ("tm", "sub")
     count = lax.axis_size(times)
-    low = lax.ppermute(raw[:, samples - margin :], times, shift_perm(count, 1))
-    high = lax.ppermute(raw[:, :margin], times, shift_perm(count, -1))
-    ext = jnp.concatenate([low, raw, high], axis=1)
     n_chan = lax.axis_size("chan")
-    below = lax.ppermute(ext[channels - side :], "chan", shift_perm(n_chan, 1))
-    above = lax.ppermute(ext[:side], "chan", shift_perm(n_chan, -1))
-    spare = jnp.zeros((16 - 2 * side, ext.shape[1]), ext.dtype)
-    ext = jnp.concatenate([ext, below, above, spare], axis=0)
-    depth = WIN + 2 * margin
-    taps = jnp.pad(fir_taps.astype(jnp.float32), (0, depth - fir_taps.shape[0]))[None, :]
+    n_tm, n_sub = lax.axis_size("tm"), lax.axis_size("sub")
+    depth = WIN + 2 * LANES
+    first = LANES - margin
+    taps = jnp.pad(fir_taps.astype(jnp.float32), (first, depth - first - fir_taps.shape[0]))[None, :]
     near, counts = smooth_table()
     white, own = pl.pallas_call(
-        functools.partial(white_kernel, frames, channels, side, steps),
+        functools.partial(white_kernel, frames, channels, side, steps, n_chan, n_tm, n_sub),
         out_shape=[
             jax.ShapeDtypeStruct((frames, channels, WIN), jnp.bfloat16),
             jax.ShapeDtypeStruct((steps, frames, P_SIZE, WIN), jnp.bfloat16),
@@ -321,14 +388,22 @@
         scratch_shapes=[
             pltpu.VMEM((2, channels + 16, WIN), jnp.float32),
             pltpu.VMEM((frames, channels, WIN), jnp.float32),
+            pltpu.VMEM((channels + 16, samples + 2 * LANES), jnp.bfloat16),
+            pltpu.VMEM((2, channels, LANES), jnp.bfloat16),
+            pltpu.VMEM((2, side, samples), jnp.bfloat16),
+            pltpu.VMEM((2, side, samples), jnp.bfloat16),
+            pltpu.VMEM((4, side, LANES), jnp.bfloat16),
+            pltpu.VMEM((4, side, LANES), jnp.bfloat16),
+            pltpu.SemaphoreType.DMA((8,)),
+            pltpu.SemaphoreType.DMA((8,)),
         ],
-        compiler_params=pltpu.CompilerParams(vmem_limit_bytes=32 * 2**20),
+        compiler_params=pltpu.CompilerParams(
+            vmem_limit_bytes=32 * 2**20, collective_id=1, has_side_effects=True),
         name="white",
-    )(taps, spatial_taps, band_edges, source_panel, ext, spectral_table(), near, jnp.asarray(counts))
+    )(taps, spatial_taps, band_edges, source_panel, raw, spectral_table(), near, jnp.asarray(counts))
 
     total = frames * count
     real, imag = lag_tables(1.0 / math.sqrt(total * (WIN // 2)))
-    n_tm, n_sub = lax.axis_size("tm"), lax.axis_size("sub")
     chunks = steps * SPLIT
     flow = pltpu.VMEM((chunks, frames // SPLIT, P_SIZE, WIN), jnp.bfloat16)
     part = channels // n_sub

time: 103 us -> 91.7 us (0.89)
  starting transfers between devices: 8.42 us -> 0 us
  waiting for transfers between devices: 7.99 us -> 0 us
  local copies, waits for them, and re-layouts: 4.93 us -> 10.5 us
    pallas_call x1, Pallas kernels: 75.1 us -> 66.2 us  [shards(): pl.pallas_call(functools.partial(cross_kernel, frames, channels, steps, n...]
    unnamed x23, local copies, waits for them, and re-layouts: 0.86 us -> 9.63 us
    ppermute x4 -> x0, starting transfers between devices: 8.42 us -> none  [the longest x1 3.48 us: shards(): below = lax.ppermute(ext[channels - side:], 'chan', shift_perm(n_chan, 1))]
    pallas_call x1, Pallas kernels: 5.44 us -> 13.7 us  [shards(): pl.pallas_call(functools.partial(white_kernel, frames, channels, side, st...]
    ppermute x4 -> x0, waiting for transfers between devices: 7.99 us -> none  [the longest x1 4.08 us: shards(): above = lax.ppermute(ext[:side], 'chan', shift_perm(n_chan, -1))]
    concatenate x2 -> x0, local copies, waits for them, and re-layouts: 2.93 us -> none  [the longest x1 2.85 us: shards(): ext = jnp.concatenate([low, raw, high], axis=1)]
  transfers between devices with their start and end apart: 4 -> 0, of which waited for: 2 -> 0; matrix products, arithmetic and copies ran while one was open for 0% -> 0% of each run, Pallas kernels for 0% -> 0%
where the time goes in v3:
time: 91.7 us; the launch traced here: 91.2 us
  Pallas kernels  79.9 us (87%)
  local copies, waits for them, and re-layouts  10.5 us (11%)
    pallas_call x1, Pallas kernels, shards(): pl.pallas_call(functools.partial(cross_kernel, frames, channels, steps, n...  66.2 us
    pallas_call x1, Pallas kernels, shards(): pl.pallas_call(functools.partial(white_kernel, frames, channels, side, st...  13.7 us
    unnamed x23, local copies, waits for them, and re-layouts  9.63 us

profile of v3, /device:TPU:0, one launch (start us, length us, event | category | flops | bytes accessed | tf_op | source)
XLA Modules:
  0.0 91.2 jit_solution(10315316036766428466)
XLA Ops:
  0.0 0.7 pad_convert_fusion
  0.7 0.9 copy.13.pick_ref
  1.6 0.0 copy-start
  1.6 1.2 %copy-done = bf16[128,4096]{1,0:T(8,128)(2,1)S(1)} copy-done((bf16[128,4096]{1,0:T(8,128)(2,1)S(1)}, bf16[128,4096]{1,0:T(8,128)(2,1)}, u32[]{:S(2)}) %copy-start) | copy-done | bytes 1048600
  2.9 0.0 copy-start.1
  2.9 0.9 %copy-done.1 = f32[256,256]{1,0:T(8,128)S(1)} copy-done((f32[256,256]{1,0:T(8,128)S(1)}, f32[256,256]{1,0:T(8,128)}, u32[]{:S(2)}) %copy-start.1) | copy-done | bytes 262168
  3.8 0.0 copy-start.4
  3.8 0.9 copy-done.4
  4.7 0.0 copy-start.5
  4.7 0.7 copy-done.5
  5.4 0.0 copy-start.7
  5.4 0.7 copy-done.7
  6.1 0.0 copy-start.8
  6.1 0.7 copy-done.8
  6.7 0.0 copy-start.9
  6.7 0.7 copy-done.9
  7.4 13.7 %white.1 = (bf16[16,128,256]{2,1,0:T(8,128)(2,1)S(1)}, bf16[8,16,32,256]{3,2,1,0:T(8,128)(2,1)S(1)}) custom-call(f32[1,512]{1,0:T(1,128)S(1)} %bitcast.2, f32[9]{0:T(128)S(1)} %copy-done.8, s32[4]{0:T(128)S(1)} %copy-done.9, s32[8]{0:T(128)S(1)} %copy-done.5, bf16[128,4096]{1,0:T(8,128)(2,1)S(1)} %copy-done, bf16[256,256]{1,0:T(8,128)(2,1)S(1)} %copy-done.4, ...), custom_call_target="tpu_custom_call" | custom-call | tf_op jit(solution)/shard_map/white/pallas_call | solution.py:380
  21.1 0.0 copy-start.2
  21.1 0.9 copy-done.2
  22.0 0.0 copy-start.3
  22.0 0.9 copy-done.3
  22.9 0.0 copy-start.6
  22.9 0.7 copy-done.6
  23.6 0.0 copy-start.10
  23.6 0.7 copy-done.10
  24.2 66.2 %cross.1 = f32[8,128,128]{2,1,0:T(8,128)S(1)} custom-call(s32[8]{0:T(128)S(1)} %copy-done.10, s32[8]{0:T(128)S(1)} %copy-done.6, s32[8,128,1]{2,1,0:T(8,128)S(1)} %copy.13.pick_ref, bf16[16,128,256]{2,1,0:T(8,128)(2,1)S(1)} %get-tuple-element.7.white_ref, bf16[8,16,32,256]{3,2,1,0:T(8,128)(2,1)S(1)} %get-tuple-element.8.own_ref, f32[256,128]{1,0:T(8,128)S(1)} %copy-done.3, ...), custom_call_target="tpu_custom_call" | custom-call | tf_op jit(solution)/shard_map/cross/pallas_call | solution.py:411
  90.4 0.8 copy.15
Async XLA Ops:
  1.6 1.2 %copy-start = (bf16[128,4096]{1,0:T(8,128)(2,1)S(1)}, bf16[128,4096]{1,0:T(8,128)(2,1)}, u32[]{:S(2)}) copy-start(bf16[128,4096]{1,0:T(8,128)(2,1)} %raw_ref.1) | copy-start | bytes 3145732
  2.9 0.9 %copy-start.1 = (f32[256,256]{1,0:T(8,128)S(1)}, f32[256,256]{1,0:T(8,128)}, u32[]{:S(2)}) copy-start(f32[256,256]{1,0:T(8,128)} %constant.14.clone.near_ref) | copy-start | bytes 786436
  3.8 0.9 copy-start.4
  4.7 0.7 copy-start.5
  5.4 0.7 copy-start.7
  6.1 0.7 copy-start.8
  6.7 0.7 copy-start.9
  21.1 0.9 copy-start.2
  22.0 0.9 copy-start.3
  22.9 0.7 copy-start.6
  23.6 0.7 copy-start.10

commit v4 on v3

--- a/solution.py
+++ b/solution.py
@@ -31,10 +31,10 @@
     return jnp.asarray(table.astype(np.float32)).astype(jnp.bfloat16)
 
 
-def smooth_table():
-    bins, _ = column_maps()
-    near = np.abs(bins[:, None] - bins[None, :]) <= 4
-    return jnp.asarray(near.astype(np.float32)), near.sum(0).astype(np.float32)[None, :] / 2.0
+def bins_of(shape, axis):
+    column = lax.broadcasted_iota(jnp.int32, shape, axis)
+    quarter = WIN // 4
+    return lax.div(column, 2 * quarter) * quarter + lax.rem(column, quarter)
 
 
 def lag_tables(scale):
@@ -43,17 +43,11 @@
     angle = 2.0 * np.pi * ((bins[:, None] * lag[None, :]) % WIN) / WIN
     real = np.cos(angle) * scale
     imag = np.where(parts[:, None] == 0, -np.sin(angle), np.sin(angle)) * scale
-    return jnp.asarray(real.astype(np.float32)), jnp.asarray(imag.astype(np.float32))
-
-
-def shift_perm(count, step):
-    return [(i, i + step) for i in range(count) if 0 <= i + step < count]
+    return jnp.asarray(np.concatenate([real, imag]).astype(np.float32))
 
 
 def taper_row(edges_ref):
-    column = lax.broadcasted_iota(jnp.int32, (1, WIN), 1)
-    quarter = WIN // 4
-    bins = (column // (2 * quarter) * quarter + column % quarter).astype(jnp.float32)
+    bins = bins_of((1, WIN), 1).astype(jnp.float32)
     e0, e1, e2, e3 = [jnp.full((1, WIN), edges_ref[k]).astype(jnp.float32) for k in range(4)]
     rising = 0.5 - 0.5 * jnp.cos(math.pi * (bins - e0) / (e1 - e0))
     falling = 0.5 - 0.5 * jnp.cos(math.pi * (e3 - bins) / (e3 - e2))
@@ -64,12 +58,25 @@
 
 
 LANES = 128
+SPLIT = 8
+LAG = 4
 MESH = pl.DeviceIdType.MESH
 
 
-def white_kernel(frames, channels, side, steps, n_chan, n_tm, n_sub, taps_ref, sp_ref, edges_ref, panel_ref,
-                 raw_ref, table_ref, near_ref, count_ref, out_ref, own_ref, filt, spec, ext, time_in,
-                 chan_out, chan_in, corner_out, corner_in, send_sem, recv_sem):
+def kernel(frames, channels, side, steps, n_chan, n_tm, n_sub, sp_ref, edges_ref, owner_ref, panel_ref,
+           taps_ref, pick_ref, raw_ref, table_hbm, lag_hbm, out_ref,
+           table_ref, lag_ref, filt, spec, ext, time_in, chan_out, chan_in, corner_out, corner_in, send_sem,
+           recv_sem, load_sem, white_ref, own_ref, chosen, pick_wide, plain, swapped, in_low, in_high, to_high,
+           to_low, own_lag, sub_in, tm_in, done, sem_high, sem_low, got_low, got_high, sub_send, sub_recv,
+           tm_send, tm_recv, fin_send, fin_recv):
+    my_tm = lax.axis_index("tm")
+    my_sub = lax.axis_index("sub")
+    loads = [
+        pltpu.make_async_copy(table_hbm, table_ref, load_sem.at[0]),
+        pltpu.make_async_copy(lag_hbm, lag_ref, load_sem.at[1]),
+    ]
+    for load in loads:
+        load.start()
     me = lax.axis_index("chan")
     n_time = n_tm * n_sub
     now = lax.axis_index("tm") * n_sub + lax.axis_index("sub")
@@ -82,8 +89,11 @@
 
     moves = [(0, 1), (0, -1), (1, 0), (-1, 0), (1, 1), (1, -1), (-1, 1), (-1, -1)]
     barrier = pltpu.get_barrier_semaphore()
-    for dc, dt in moves:
-        pl.semaphore_signal(barrier, inc=1, device_id=peer(dc, dt), device_id_type=MESH)
+    peers = [peer(dc, dt) for dc, dt in moves]
+    peers += [{"tm": lax.rem(my_tm + d, n_tm)} for d in range(1, n_tm)]
+    peers += [{"sub": lax.rem(my_sub + d, n_sub)} for d in range(1, n_sub)]
+    for to in peers:
+        pl.semaphore_signal(barrier, inc=1, device_id=to, device_id_type=MESH)
 
     ends = (slice(channels - side, channels), slice(0, side))
     sides = (slice(samples - LANES, samples), slice(0, LANES))
@@ -107,13 +117,31 @@
             src_ref=src, dst_ref=dst, send_sem=send_sem.at[k], recv_sem=recv_sem.at[k],
             device_id=peer(dc, dt), device_id_type=MESH)
 
-    pl.semaphore_wait(barrier, len(moves))
+    pl.semaphore_wait(barrier, len(peers))
     for k in (2, 3, 0, 1, 4, 5, 6, 7):
         pl.when(exists(*moves[k]))(lambda k=k: copy(k).start())
 
     ext[:channels, LANES : LANES + samples] = raw_ref[...]
     rolled = pltpu.roll(jnp.broadcast_to(taps_ref[...], (WIN, depth)), 0, 1, stride=1, stride_axis=0)
     fir_t = rolled.astype(jnp.bfloat16)
+    near = (jnp.abs(bins_of((WIN, WIN), 0) - bins_of((WIN, WIN), 1)) <= 4).astype(jnp.float32)
+    row_bins = bins_of((1, WIN), 1)
+    count = jnp.minimum(row_bins + 4, WIN // 2 - 1) - jnp.maximum(row_bins - 4, 0) + 1
+    turned = jnp.transpose(pick_ref[...].astype(jnp.float32))
+    for s in range(steps):
+        wide = jnp.broadcast_to(turned[:, s : s + 1], (channels, LANES)).astype(jnp.int32)
+        pick_wide[s] = wide
+        chosen[s] = (
+            wide[:, :P_SIZE] == lax.broadcasted_iota(jnp.int32, (channels, P_SIZE), 1)
+        ).astype(jnp.bfloat16)
+
+    @pl.when(me == 0)
+    def _():
+        in_low[...] = jnp.zeros_like(in_low)
+
+    @pl.when(me == n_chan - 1)
+    def _():
+        in_high[...] = jnp.zeros_like(in_high)
 
     for k, (dc, dt) in enumerate(moves):
         there = exists(-dc, -dt)
@@ -136,6 +164,7 @@
     ext[channels:, LANES:high_at] = rows(chan_in[0], chan_in[1])
     ext[channels:, :LANES] = rows(corner_in[0], corner_in[2])
     ext[channels:, high_at:] = rows(corner_in[1], corner_in[3])
+    loads[0].wait()
     power = jnp.zeros((channels, WIN), jnp.float32)
     for w in range(frames):
         block = ext[:, w * WIN : w * WIN + depth]
@@ -150,46 +179,17 @@
         spectra = jnp.dot(shaped.astype(jnp.bfloat16), table_ref[...], preferred_element_type=jnp.float32)
         spec[w] = spectra
         power += spectra * spectra
-    level = jnp.dot(power, near_ref[...], precision=HIGHEST, preferred_element_type=jnp.float32)
-    level = level / (count_ref[...] * frames)
+    level = jnp.dot(power, near, precision=HIGHEST, preferred_element_type=jnp.float32)
+    level = level / (count.astype(jnp.float32) * frames)
     factor = taper_row(edges_ref) / jnp.sqrt(level + 1e-06)
     for w in range(frames):
-        out_ref[w] = (spec[w] * factor).astype(jnp.bfloat16)
-    for s in range(steps):
-        panel = jnp.full((P_SIZE, WIN), panel_ref[s], jnp.int32)
-        for w in range(frames):
-            value = out_ref[w, :P_SIZE]
-            for k in range(1, channels // P_SIZE):
-                value = jnp.where(panel == k, out_ref[w, k * P_SIZE : (k + 1) * P_SIZE], value)
-            own_ref[s, w] = value
-    for k, move in enumerate(moves):
-        pl.when(exists(*move))(lambda k=k: copy(k).wait_send())
-
-
-SPLIT = 4
-LAG = 3
-
-
-def cross_kernel(frames, channels, steps, n_chan, n_tm, n_sub, owner_ref, panel_ref, pick_ref, white_ref, own_ref,
-                 real_ref, imag_ref, out_ref, plain, swapped, in_low, in_high, to_high, to_low, own_lag,
-                 sub_in, tm_in, done, sem_high, sem_low, got_low, got_high, sub_send, sub_recv,
-                 tm_send, tm_recv, fin_send, fin_recv):
-    me = lax.axis_index("chan")
-    my_tm = lax.axis_index("tm")
-    my_sub = lax.axis_index("sub")
+        white_ref[w] = (spec[w] * factor).astype(jnp.bfloat16)
+    loads[1].wait()
     half = WIN // 2
     part = channels // n_sub
     group = frames // SPLIT
     chunks = steps * SPLIT
 
-    barrier = pltpu.get_barrier_semaphore()
-    peers = [{"chan": lax.rem(me + d, n_chan)} for d in (1, n_chan - 1)]
-    peers += [{"tm": lax.rem(my_tm + d, n_tm)} for d in range(1, n_tm)]
-    peers += [{"sub": lax.rem(my_sub + d, n_sub)} for d in range(1, n_sub)]
-    for peer in peers:
-        pl.semaphore_signal(barrier, inc=1, device_id=peer, device_id_type=MESH)
-    pl.semaphore_wait(barrier, len(peers))
-
     def up(c):
         return pltpu.make_async_remote_copy(
             src_ref=to_high.at[c], dst_ref=in_low.at[c], send_sem=sem_high.at[c], recv_sem=got_low.at[c],
@@ -220,13 +220,13 @@
             send_sem=fin_send.at[s, d - 1], recv_sem=fin_recv.at[s, d - 1],
             device_id={"sub": lax.rem(my_sub + d, n_sub)}, device_id_type=MESH)
 
-    @pl.when(me == 0)
-    def _():
-        in_low[...] = jnp.zeros_like(in_low)
-
-    @pl.when(me == n_chan - 1)
-    def _():
-        in_high[...] = jnp.zeros_like(in_high)
+    def own_panel(s):
+        panel = jnp.full((P_SIZE, WIN), panel_ref[s], jnp.int32)
+        for w in range(frames):
+            value = white_ref[w, :P_SIZE]
+            for k in range(1, channels // P_SIZE):
+                value = jnp.where(panel == k, white_ref[w, k * P_SIZE : (k + 1) * P_SIZE], value)
+            own_ref[s, w] = value
 
     def stage(c, arrived, leaving):
         s = lax.div(c, SPLIT)
@@ -267,10 +267,6 @@
         owner = owner_ref[s]
         where = jnp.full((P_SIZE, WIN), owner, jnp.int32)
         start = owner * channels + panel_ref[s] * P_SIZE
-        chosen = []
-        for r in range(2):
-            pick = pick_ref[s, r * rows : (r + 1) * rows]
-            chosen.append((pick == lax.broadcasted_iota(jnp.int32, (rows, P_SIZE), 1)).astype(jnp.bfloat16))
         for r in range(2):
             here = slice(r * rows, (r + 1) * rows)
             acc_p = jnp.zeros((rows, WIN), jnp.float32)
@@ -279,13 +275,13 @@
                 c = s * SPLIT + w // group
                 value = jnp.where(where < me, in_low[c, w % group], in_high[c, w % group])
                 value = jnp.where(where == me, own_ref[s, w], value)
-                partner = jnp.dot(chosen[r], value, preferred_element_type=jnp.float32)
+                partner = jnp.dot(chosen[s, here], value, preferred_element_type=jnp.float32)
                 acc_p += plain[w, here] * partner
                 acc_q += swapped[w, here] * partner
-            lagged = jnp.dot(acc_p, real_ref[...], precision=HIGHEST, preferred_element_type=jnp.float32)
-            lagged += jnp.dot(acc_q, imag_ref[...], precision=HIGHEST, preferred_element_type=jnp.float32)
-            receiver = me * channels + r * rows + lax.broadcasted_iota(jnp.int32, (rows, 1), 0)
-            far = jnp.abs(receiver - (start + pick_ref[s, here])) > REACH
+            lagged = jnp.dot(acc_p, lag_ref[:WIN], precision=HIGHEST, preferred_element_type=jnp.float32)
+            lagged += jnp.dot(acc_q, lag_ref[WIN:], precision=HIGHEST, preferred_element_type=jnp.float32)
+            receiver = me * channels + r * rows + lax.broadcasted_iota(jnp.int32, (rows, LAGS), 0)
+            far = jnp.abs(receiver - (start + pick_wide[s, here])) > REACH
             own_lag[s, here] = jnp.where(far, 0.0, lagged)
         for d in range(1, n_sub):
             sub_copy(s, d).start()
@@ -317,6 +313,7 @@
     delay = -(-(n_chan - 1) * LAG // SPLIT)
 
     def turn(u, carry):
+        pl.when(u < steps)(functools.partial(own_panel, u))
         for k in range(SPLIT):
             relay(u * SPLIT + k)
 
@@ -347,6 +344,8 @@
         return carry
 
     lax.fori_loop(0, chunks, drain_chunk, 0)
+    for k, move in enumerate(moves):
+        pl.when(exists(*move))(lambda k=k: copy(k).wait_send())
 
     def drain_step(s, carry):
         for d in range(1, n_sub):
@@ -376,60 +375,51 @@
     depth = WIN + 2 * LANES
     first = LANES - margin
     taps = jnp.pad(fir_taps.astype(jnp.float32), (first, depth - first - fir_taps.shape[0]))[None, :]
-    near, counts = smooth_table()
-    white, own = pl.pallas_call(
-        functools.partial(white_kernel, frames, channels, side, steps, n_chan, n_tm, n_sub),
-        out_shape=[
-            jax.ShapeDtypeStruct((frames, channels, WIN), jnp.bfloat16),
-            jax.ShapeDtypeStruct((steps, frames, P_SIZE, WIN), jnp.bfloat16),
-        ],
-        in_specs=[VMEM, SMEM, SMEM, SMEM, VMEM, VMEM, VMEM, VMEM],
-        out_specs=[VMEM, VMEM],
-        scratch_shapes=[
-            pltpu.VMEM((2, channels + 16, WIN), jnp.float32),
-            pltpu.VMEM((frames, channels, WIN), jnp.float32),
-            pltpu.VMEM((channels + 16, samples + 2 * LANES), jnp.bfloat16),
-            pltpu.VMEM((2, channels, LANES), jnp.bfloat16),
-            pltpu.VMEM((2, side, samples), jnp.bfloat16),
-            pltpu.VMEM((2, side, samples), jnp.bfloat16),
-            pltpu.VMEM((4, side, LANES), jnp.bfloat16),
-            pltpu.VMEM((4, side, LANES), jnp.bfloat16),
-            pltpu.SemaphoreType.DMA((8,)),
-            pltpu.SemaphoreType.DMA((8,)),
-        ],
-        compiler_params=pltpu.CompilerParams(
-            vmem_limit_bytes=32 * 2**20, collective_id=1, has_side_effects=True),
-        name="white",
-    )(taps, spatial_taps, band_edges, source_panel, raw, spectral_table(), near, jnp.asarray(counts))
-
-    total = frames * count
-    real, imag = lag_tables(1.0 / math.sqrt(total * (WIN // 2)))
+    total = frames * n_tm * n_sub
+    lag_table = lag_tables(1.0 / math.sqrt(total * (WIN // 2)))
     chunks = steps * SPLIT
     flow = pltpu.VMEM((chunks, frames // SPLIT, P_SIZE, WIN), jnp.bfloat16)
     part = channels // n_sub
     dma = pltpu.SemaphoreType.DMA
+    any_space = pl.BlockSpec(memory_space=pl.ANY)
+    bf16, f32 = jnp.bfloat16, jnp.float32
     return pl.pallas_call(
-        functools.partial(cross_kernel, frames, channels, steps, n_chan, n_tm, n_sub),
-        out_shape=jax.ShapeDtypeStruct((steps, channels, LAGS), jnp.float32),
-        in_specs=[SMEM, SMEM, VMEM, VMEM, VMEM, VMEM, VMEM],
+        functools.partial(kernel, frames, channels, side, steps, n_chan, n_tm, n_sub),
+        out_shape=jax.ShapeDtypeStruct((steps, channels, LAGS), f32),
+        in_specs=[SMEM, SMEM, SMEM, SMEM, VMEM, VMEM, VMEM, any_space, any_space],
         out_specs=VMEM,
         scratch_shapes=[
-            pltpu.VMEM((frames, channels, WIN), jnp.float32),
-            pltpu.VMEM((frames, channels, WIN), jnp.float32),
+            pltpu.VMEM((WIN, WIN), bf16),
+            pltpu.VMEM((2 * WIN, LAGS), f32),
+            pltpu.VMEM((2, channels + 16, WIN), f32),
+            pltpu.VMEM((frames, channels, WIN), f32),
+            pltpu.VMEM((channels + 16, samples + 2 * LANES), bf16),
+            pltpu.VMEM((2, channels, LANES), bf16),
+            pltpu.VMEM((2, side, samples), bf16),
+            pltpu.VMEM((2, side, samples), bf16),
+            pltpu.VMEM((4, side, LANES), bf16),
+            pltpu.VMEM((4, side, LANES), bf16),
+            dma((8,)), dma((8,)), dma((2,)),
+            pltpu.VMEM((frames, channels, WIN), bf16),
+            pltpu.VMEM((steps, frames, P_SIZE, WIN), bf16),
+            pltpu.VMEM((steps, channels, P_SIZE), bf16),
+            pltpu.VMEM((steps, channels, LANES), jnp.int32),
+            pltpu.VMEM((frames, channels, WIN), f32),
+            pltpu.VMEM((frames, channels, WIN), f32),
             flow, flow, flow, flow,
-            pltpu.VMEM((steps, channels, LAGS), jnp.float32),
-            pltpu.VMEM((steps, n_sub - 1, part, LAGS), jnp.float32),
-            pltpu.VMEM((steps, n_tm, part, LAGS), jnp.float32),
-            pltpu.VMEM((steps, channels, LAGS), jnp.float32),
+            pltpu.VMEM((steps, channels, LAGS), f32),
+            pltpu.VMEM((steps, n_sub - 1, part, LAGS), f32),
+            pltpu.VMEM((steps, n_tm, part, LAGS), f32),
+            pltpu.VMEM((steps, channels, LAGS), f32),
             dma((chunks,)), dma((chunks,)), dma((chunks,)), dma((chunks,)),
             dma((steps, n_sub - 1)), dma((steps, n_sub - 1)),
             dma((steps, n_tm - 1)), dma((steps, n_tm - 1)),
             dma((steps, n_sub - 1)), dma((steps, n_sub - 1)),
         ],
         compiler_params=pltpu.CompilerParams(
-            vmem_limit_bytes=40 * 2**20, collective_id=0, has_side_effects=True),
-        name="cross",
-    )(source_owner, source_panel, source_pick[:, :, None], white, own, real, imag)
+            vmem_limit_bytes=48 * 2**20, collective_id=0, has_side_effects=True),
+        name="correlate",
+    )(spatial_taps, band_edges, source_owner, source_panel, taps, source_pick, raw, spectral_table(), lag_table)
 
 
 def solution(mesh):

time: 91.7 us -> 88.9 us (0.969)
  local copies, waits for them, and re-layouts: 10.5 us -> 6.5 us
  Pallas kernels: 79.9 us -> 81.4 us
    unnamed x23 -> x17, local copies, waits for them, and re-layouts: 9.63 us -> 6.5 us
    pallas_call x2 -> x1, Pallas kernels: 79.9 us -> 81.4 us  [shards(): pl.pallas_call(functools.partial(kernel, frames, channels, side, steps, n...]
where the time goes in v4:
time: 88.9 us; the launch traced here: 88.7 us
  Pallas kernels  81.4 us (92%)
  local copies, waits for them, and re-layouts  6.5 us (7%)
    pallas_call x1, Pallas kernels, shards(): pl.pallas_call(functools.partial(kernel, frames, channels, side, steps, n...  81.4 us
    unnamed x17, local copies, waits for them, and re-layouts  6.5 us

profile of v4, /device:TPU:0, one launch (start us, length us, event | category | flops | bytes accessed | tf_op | source)
XLA Modules:
  0.0 88.7 jit_solution(2522511425606090580)
XLA Ops:
  0.0 0.0 copy-start.3
  0.0 0.7 pad_convert_fusion
  0.7 0.0 copy-done.3
  0.7 0.0 copy-start
  0.7 1.2 %copy-done = bf16[128,4096]{1,0:T(8,128)(2,1)S(1)} copy-done((bf16[128,4096]{1,0:T(8,128)(2,1)S(1)}, bf16[128,4096]{1,0:T(8,128)(2,1)}, u32[]{:S(2)}) %copy-start) | copy-done | bytes 1048600
  2.0 0.0 copy-start.1
  2.0 0.9 %copy-done.1 = f32[512,128]{1,0:T(8,128)S(1)} copy-done((f32[512,128]{1,0:T(8,128)S(1)}, f32[512,128]{1,0:T(8,128)}, u32[]{:S(2)}) %copy-start.1) | copy-done | bytes 262168
  2.9 0.0 copy-start.2
  2.9 0.9 %copy-done.2 = bf16[256,256]{1,0:T(8,128)(2,1)S(1)} copy-done((bf16[256,256]{1,0:T(8,128)(2,1)S(1)}, bf16[256,256]{1,0:T(8,128)(2,1)}, u32[]{:S(2)}) %copy-start.2) | copy-done | bytes 131096
  3.8 0.0 copy-start.4
  3.8 0.7 copy-done.4
  4.5 0.0 copy-start.5
  4.5 0.7 copy-done.5
  5.1 0.0 copy-start.6
  5.1 0.7 copy-done.6
  5.8 0.0 copy-start.7
  5.8 0.7 copy-done.7
  6.5 81.4 %correlate.1 = f32[8,128,128]{2,1,0:T(8,128)S(1)} custom-call(f32[9]{0:T(128)S(1)} %copy-done.4, s32[4]{0:T(128)S(1)} %copy-done.5, s32[8]{0:T(128)S(1)} %copy-done.6, s32[8]{0:T(128)S(1)} %copy-done.7, f32[1,512]{1,0:T(1,128)S(1)} %bitcast.1, s32[8,128]{1,0:T(8,128)S(1)} %copy-done.3, bf16[128,4096]{1,0:T(8,128)(2,1)S(1)} %copy-done, ...), custom_call_target="tpu_custom_call" | custom-call | tf_op jit(solution)/shard_map/correlate/pallas_call | solution.py:386
  87.9 0.8 copy.11
Async XLA Ops:
  0.0 0.7 copy-start.3
  0.7 1.2 %copy-start = (bf16[128,4096]{1,0:T(8,128)(2,1)S(1)}, bf16[128,4096]{1,0:T(8,128)(2,1)}, u32[]{:S(2)}) copy-start(bf16[128,4096]{1,0:T(8,128)(2,1)} %raw_ref.1) | copy-start | bytes 3145732
  2.0 0.9 %copy-start.1 = (f32[512,128]{1,0:T(8,128)S(1)}, f32[512,128]{1,0:T(8,128)}, u32[]{:S(2)}) copy-start(f32[512,128]{1,0:T(8,128)} %constant.8.clone.lag_hbm) | copy-start | bytes 786436
  2.9 0.9 %copy-start.2 = (bf16[256,256]{1,0:T(8,128)(2,1)S(1)}, bf16[256,256]{1,0:T(8,128)(2,1)}, u32[]{:S(2)}) copy-start(bf16[256,256]{1,0:T(8,128)(2,1)} %constant.12.table_hbm) | copy-start | bytes 393220
  3.8 0.7 copy-start.4
  4.5 0.7 copy-start.5
  5.1 0.7 copy-start.6
  5.8 0.7 copy-start.7

commit v5 on v4

--- a/solution.py
+++ b/solution.py
@@ -58,22 +58,26 @@
 
 
 LANES = 128
-SPLIT = 8
-LAG = 4
+SPLIT = 2
+LAG = 2
 MESH = pl.DeviceIdType.MESH
 
 
-def kernel(frames, channels, side, steps, n_chan, n_tm, n_sub, sp_ref, edges_ref, owner_ref, panel_ref,
-           taps_ref, pick_ref, raw_ref, table_hbm, lag_hbm, out_ref,
-           table_ref, lag_ref, filt, spec, ext, time_in, chan_out, chan_in, corner_out, corner_in, send_sem,
+def kernel(frames, channels, side, steps, n_chan, n_tm, n_sub, sp_hbm, edges_hbm, owner_hbm, panel_hbm,
+           taps_hbm, pick_hbm, raw_hbm, table_hbm, lag_hbm, out_ref,
+           sp_ref, edges_ref, owner_ref, panel_ref, taps_ref, pick_ref, raw_ref, table_ref, lag_ref, filt, spec, ext, time_in, chan_out, chan_in, corner_out, corner_in, send_sem,
            recv_sem, load_sem, white_ref, own_ref, chosen, pick_wide, plain, swapped, in_low, in_high, to_high,
            to_low, own_lag, sub_in, tm_in, done, sem_high, sem_low, got_low, got_high, sub_send, sub_recv,
            tm_send, tm_recv, fin_send, fin_recv):
     my_tm = lax.axis_index("tm")
     my_sub = lax.axis_index("sub")
     loads = [
-        pltpu.make_async_copy(table_hbm, table_ref, load_sem.at[0]),
-        pltpu.make_async_copy(lag_hbm, lag_ref, load_sem.at[1]),
+        pltpu.make_async_copy(source, target, load_sem.at[k])
+        for k, (source, target) in enumerate([
+            (raw_hbm, raw_ref), (taps_hbm, taps_ref), (pick_hbm, pick_ref), (sp_hbm, sp_ref),
+            (edges_hbm, edges_ref), (owner_hbm, owner_ref), (panel_hbm, panel_ref),
+            (table_hbm, table_ref), (lag_hbm, lag_ref),
+        ])
     ]
     for load in loads:
         load.start()
@@ -95,6 +99,7 @@
     for to in peers:
         pl.semaphore_signal(barrier, inc=1, device_id=to, device_id_type=MESH)
 
+    loads[0].wait()
     ends = (slice(channels - side, channels), slice(0, side))
     sides = (slice(samples - LANES, samples), slice(0, LANES))
     for k in range(2):
@@ -122,6 +127,8 @@
         pl.when(exists(*moves[k]))(lambda k=k: copy(k).start())
 
     ext[:channels, LANES : LANES + samples] = raw_ref[...]
+    for load in loads[1:]:
+        load.wait()
     rolled = pltpu.roll(jnp.broadcast_to(taps_ref[...], (WIN, depth)), 0, 1, stride=1, stride_axis=0)
     fir_t = rolled.astype(jnp.bfloat16)
     near = (jnp.abs(bins_of((WIN, WIN), 0) - bins_of((WIN, WIN), 1)) <= 4).astype(jnp.float32)
@@ -164,7 +171,6 @@
     ext[channels:, LANES:high_at] = rows(chan_in[0], chan_in[1])
     ext[channels:, :LANES] = rows(corner_in[0], corner_in[2])
     ext[channels:, high_at:] = rows(corner_in[1], corner_in[3])
-    loads[0].wait()
     power = jnp.zeros((channels, WIN), jnp.float32)
     for w in range(frames):
         block = ext[:, w * WIN : w * WIN + depth]
@@ -184,7 +190,6 @@
     factor = taper_row(edges_ref) / jnp.sqrt(level + 1e-06)
     for w in range(frames):
         white_ref[w] = (spec[w] * factor).astype(jnp.bfloat16)
-    loads[1].wait()
     half = WIN // 2
     part = channels // n_sub
     group = frames // SPLIT
@@ -358,7 +363,6 @@
     lax.fori_loop(0, steps, drain_step, 0)
 
 
-SMEM = pl.BlockSpec(memory_space=pltpu.SMEM)
 VMEM = pl.BlockSpec(memory_space=pltpu.VMEM)
 
 
@@ -386,9 +390,16 @@
     return pl.pallas_call(
         functools.partial(kernel, frames, channels, side, steps, n_chan, n_tm, n_sub),
         out_shape=jax.ShapeDtypeStruct((steps, channels, LAGS), f32),
-        in_specs=[SMEM, SMEM, SMEM, SMEM, VMEM, VMEM, VMEM, any_space, any_space],
+        in_specs=[any_space] * 9,
         out_specs=VMEM,
         scratch_shapes=[
+            pltpu.SMEM(spatial_taps.shape, f32),
+            pltpu.SMEM(band_edges.shape, jnp.int32),
+            pltpu.SMEM(source_owner.shape, jnp.int32),
+            pltpu.SMEM(source_panel.shape, jnp.int32),
+            pltpu.VMEM(taps.shape, f32),
+            pltpu.VMEM(source_pick.shape, jnp.int32),
+            pltpu.VMEM(raw.shape, bf16),
             pltpu.VMEM((WIN, WIN), bf16),
             pltpu.VMEM((2 * WIN, LAGS), f32),
             pltpu.VMEM((2, channels + 16, WIN), f32),
@@ -399,7 +410,7 @@
             pltpu.VMEM((2, side, samples), bf16),
             pltpu.VMEM((4, side, LANES), bf16),
             pltpu.VMEM((4, side, LANES), bf16),
-            dma((8,)), dma((8,)), dma((2,)),
+            dma((8,)), dma((8,)), dma((9,)),
             pltpu.VMEM((frames, channels, WIN), bf16),
             pltpu.VMEM((steps, frames, P_SIZE, WIN), bf16),
             pltpu.VMEM((steps, channels, P_SIZE), bf16),

time: 88.9 us -> 84 us (0.945)
  Pallas kernels: 81.4 us -> 76.3 us
    pallas_call x1, Pallas kernels: 81.4 us -> 76.3 us  [shards(): pl.pallas_call(functools.partial(kernel, frames, channels, side, steps, n...]
where the time goes in v5:
time: 84 us; the launch traced here: 83.5 us
  Pallas kernels  76.3 us (91%)
  local copies, waits for them, and re-layouts  6.5 us (8%)
    pallas_call x1, Pallas kernels, shards(): pl.pallas_call(functools.partial(kernel, frames, channels, side, steps, n...  76.3 us
    unnamed x17, local copies, waits for them, and re-layouts  6.5 us

profile of v5, /device:TPU:0, one launch (start us, length us, event | category | flops | bytes accessed | tf_op | source)
XLA Modules:
  0.0 83.5 jit_solution(9307545845274131106)
XLA Ops:
  0.0 0.0 copy-start.3
  0.0 0.7 pad_convert_fusion
  0.7 0.0 copy-done.3
  0.7 0.0 copy-start
  0.7 1.2 %copy-done = bf16[128,4096]{1,0:T(8,128)(2,1)S(1)} copy-done((bf16[128,4096]{1,0:T(8,128)(2,1)S(1)}, bf16[128,4096]{1,0:T(8,128)(2,1)}, u32[]{:S(2)}) %copy-start) | copy-done | bytes 1048600
  2.0 0.0 copy-start.1
  2.0 0.9 %copy-done.1 = f32[512,128]{1,0:T(8,128)S(1)} copy-done((f32[512,128]{1,0:T(8,128)S(1)}, f32[512,128]{1,0:T(8,128)}, u32[]{:S(2)}) %copy-start.1) | copy-done | bytes 262168
  2.9 0.0 copy-start.2
  2.9 0.9 %copy-done.2 = bf16[256,256]{1,0:T(8,128)(2,1)S(1)} copy-done((bf16[256,256]{1,0:T(8,128)(2,1)S(1)}, bf16[256,256]{1,0:T(8,128)(2,1)}, u32[]{:S(2)}) %copy-start.2) | copy-done | bytes 131096
  3.8 0.0 copy-start.4
  3.8 0.7 copy-done.4
  4.5 0.0 copy-start.5
  4.5 0.7 copy-done.5
  5.1 0.0 copy-start.6
  5.1 0.7 copy-done.6
  5.8 0.0 copy-start.7
  5.8 0.7 copy-done.7
  6.5 76.3 %correlate.1 = f32[8,128,128]{2,1,0:T(8,128)S(1)} custom-call(f32[9]{0:T(128)S(1)} %copy-done.4, s32[4]{0:T(128)S(1)} %copy-done.5, s32[8]{0:T(128)S(1)} %copy-done.6, s32[8]{0:T(128)S(1)} %copy-done.7, f32[1,512]{1,0:T(1,128)S(1)} %bitcast.1, s32[8,128]{1,0:T(8,128)S(1)} %copy-done.3, bf16[128,4096]{1,0:T(8,128)(2,1)S(1)} %copy-done, ...), custom_call_target="tpu_custom_call" | custom-call | tf_op jit(solution)/shard_map/correlate/pallas_call | solution.py:390
  82.7 0.8 copy.11
Async XLA Ops:
  0.0 0.7 copy-start.3
  0.7 1.2 %copy-start = (bf16[128,4096]{1,0:T(8,128)(2,1)S(1)}, bf16[128,4096]{1,0:T(8,128)(2,1)}, u32[]{:S(2)}) copy-start(bf16[128,4096]{1,0:T(8,128)(2,1)} %raw_hbm.1) | copy-start | bytes 3145732
  2.0 0.9 %copy-start.1 = (f32[512,128]{1,0:T(8,128)S(1)}, f32[512,128]{1,0:T(8,128)}, u32[]{:S(2)}) copy-start(f32[512,128]{1,0:T(8,128)} %constant.8.clone.lag_hbm) | copy-start | bytes 786436
  2.9 0.9 %copy-start.2 = (bf16[256,256]{1,0:T(8,128)(2,1)S(1)}, bf16[256,256]{1,0:T(8,128)(2,1)}, u32[]{:S(2)}) copy-start(bf16[256,256]{1,0:T(8,128)(2,1)} %constant.12.table_hbm) | copy-start | bytes 393220
  3.8 0.7 copy-start.4
  4.5 0.7 copy-start.5
  5.1 0.7 copy-start.6
  5.8 0.7 copy-start.7

commit v6 on v5

--- a/solution.py
+++ b/solution.py
@@ -385,7 +385,7 @@
     flow = pltpu.VMEM((chunks, frames // SPLIT, P_SIZE, WIN), jnp.bfloat16)
     part = channels // n_sub
     dma = pltpu.SemaphoreType.DMA
-    any_space = pl.BlockSpec(memory_space=pl.ANY)
+    any_space = pl.BlockSpec(memory_space=pltpu.HBM)
     bf16, f32 = jnp.bfloat16, jnp.float32
     return pl.pallas_call(
         functools.partial(kernel, frames, channels, side, steps, n_chan, n_tm, n_sub),
@@ -428,7 +428,7 @@
             dma((steps, n_sub - 1)), dma((steps, n_sub - 1)),
         ],
         compiler_params=pltpu.CompilerParams(
-            vmem_limit_bytes=48 * 2**20, collective_id=0, has_side_effects=True),
+            vmem_limit_bytes=64 * 2**20, collective_id=0, has_side_effects=True),
         name="correlate",
     )(spatial_taps, band_edges, source_owner, source_panel, taps, source_pick, raw, spectral_table(), lag_table)
 

time: 84 us -> 80.3 us (0.956)
  local copies, waits for them, and re-layouts: 6.5 us -> 1.87 us
    unnamed x17 -> x1, local copies, waits for them, and re-layouts: 6.5 us -> 1.87 us
where the time goes in v6:
time: 80.3 us; the launch traced here: 79.9 us
  Pallas kernels  76.7 us (96%)
  local copies, waits for them, and re-layouts  1.87 us (2%)
  other arithmetic  1.3 us (2%)
    pallas_call x1, Pallas kernels, shards(): pl.pallas_call(functools.partial(kernel, frames, channels, side, steps, n...  76.7 us
    unnamed x1, local copies, waits for them, and re-layouts  1.87 us

profile of v6, /device:TPU:0, one launch (start us, length us, event | category | flops | bytes accessed | tf_op | source)
XLA Modules:
  0.0 79.9 jit_solution(10994066265773285026)
XLA Ops:
  0.0 1.3 %pad_convert_fusion = f32[512]{0:T(512)} fusion(bf16[129]{0:T(256)(128)(2,1)} %param.10), kind=kLoop, calls=%fused_computation | loop fusion | flops 512 | bytes 2306 | tf_op jit(solution)/shard_map/broadcast_in_dim | solution.py:381
  1.3 76.7 %correlate.1 = f32[8,128,128]{2,1,0:T(8,128)} custom-call(f32[9]{0:T(128)} %sp_hbm.1, s32[4]{0:T(128)} %edges_hbm.1, s32[8]{0:T(128)} %owner_hbm.1, s32[8]{0:T(128)} %panel_hbm.1, f32[1,512]{1,0:T(1,128)} %bitcast.1, s32[8,128]{1,0:T(8,128)} %pick_hbm.1, bf16[128,4096]{1,0:T(8,128)(2,1)} %raw_hbm.1, bf16[256,256]{1,0:T(8,128)(2,1)} %constant.12.table_hbm, ...), custom_call_target="tpu_custom_call" | custom-call | tf_op jit(solution)/shard_map/correlate/pallas_call | solution.py:390
  78.1 1.9 %copy.11 = f32[8,128,128]{2,1,0:T(8,128)} copy(f32[8,128,128]{2,1,0:T(8,128)} %correlate.1) | data formatting | bytes 1048576
